TPU v7x, 32 devices: a whole 2x2x4 slice. The times are simulated.
32 devices in a mesh: dp: 8 (over z, y), tensor: 4 (over x, core).
Axes of the slice: x: 2, y: 2, z: 4, core: 2. Of those that a mesh axis runs over, the one named last changes fastest.
Arguments:
- hidden_in: bfloat16 [16384, 768], P(('dp', 'tensor')), may hold values from -6 to 6
- earlier: bfloat16 [4, 16384, 768], P(None, ('dp', 'tensor')), may hold values from -6 to 6
- gain_attn: float32 [768], replicated, may hold values from 0.1 to 1.9
- gain_mlp: float32 [768], replicated, may hold values from 0.1 to 1.9
- w_qkv: bfloat16 [768, 3, 768], P('dp', None, 'tensor'), may hold values from -0.21875 to 0.21875
- w_out: bfloat16 [768, 768], P('tensor', 'dp'), may hold values from -1.75 to 1.75
- w_up: bfloat16 [768, 3072], P('dp', 'tensor'), may hold values from -0.21875 to 0.21875
- w_down: bfloat16 [3072, 768], P('tensor', 'dp'), may hold values from -0.109375 to 0.109375
- mix_weights: float32 [5], replicated, may hold values from 0.3 to 1.2
- lengths: int32 [16, 4], P('dp'), may hold values from 0 to 1024, as said below
- slot_perm: int32 [16384], P('dp'), may hold values from 0 to 2047, as said below
- grad_out: bfloat16 [16384, 768], P(('dp', 'tensor')), may hold values from -6 to 6
Outputs:
- mixed_out: bfloat16 [16384, 768], P(('dp', 'tensor'))
- grad_hidden: bfloat16 [16384, 768], P(('dp', 'tensor'))
- grad_earlier: bfloat16 [4, 16384, 768], P(None, ('dp', 'tensor'))
- grad_gain_attn: float32 [768], replicated
- grad_gain_mlp: float32 [768], replicated
- grad_w_qkv: float32 [768, 3, 768], P('dp', None, 'tensor')
- grad_w_out: float32 [768, 768], P('tensor', 'dp')
- grad_w_up: float32 [768, 3072], P('dp', 'tensor')
- grad_w_down: float32 [3072, 768], P('tensor', 'dp')
- grad_mix: float32 [5], replicated
Inputs may be any that keep to these rules, and one draw needn't show every extreme that they name: Each slot's lengths sum to at most 1024; in every draw some slot holds one sequence of exactly 1024 and entries of 0 there. `slot_perm`: each aligned block of 2048 entries holds every number of 0 to 2047 once.
All inputs are finite; a program needn't handle non-finite values.
Results may differ from a plain program's by a relative error of at most 0.013.
The roundings to bfloat16 on the way count: a program that leaves them out, or rounds other values in their place, can miss the bound.
Values may be sent and summed in bfloat16 or wider, within the bound.
No kernel may reach another device: no remote copies, remote signals or barrier semaphores. Data moves between devices by JAX's collectives and lax.ppermute only.
A program may use at most 192 MiB of HBM per device.

v0:
```python
import jax
import jax.numpy as jnp
from jax import lax
from jax.sharding import PartitionSpec as P

HEAD_SIZE = 64


eps = 1e-05


def layer_norm(value, gain):
    row_mean = jnp.mean(value, axis=-1, keepdims=True)
    centered = value - row_mean
    spread = jnp.mean(centered * centered, axis=-1, keepdims=True)
    return centered * lax.rsqrt(spread + eps) * gain


def slot_layout(lengths, slot_len):
    ends = jnp.cumsum(lengths, axis=-1)
    starts = ends - lengths
    places = jnp.arange(slot_len, dtype=jnp.int32)
    segment = jnp.sum((places[None, :, None] >= ends[:, None, :]).astype(jnp.int32), axis=-1)
    begins = jnp.concatenate([starts, ends[:, -1:]], axis=1)
    first = jnp.take_along_axis(begins, segment, axis=1)
    return (segment, places[None, :] - first)


def angles(position, head_width):
    half_width = head_width // 2
    inverse = 1.0 / 10000.0 ** (jnp.arange(half_width, dtype=jnp.float32) * (2.0 / head_width))
    phase_angle = position.astype(jnp.float32)[:, None] * inverse[None, :]
    return (jnp.cos(phase_angle)[:, None, :], jnp.sin(phase_angle)[:, None, :])


def rotate(value, cosine, sine):
    half_width = value.shape[-1] // 2
    first = value[..., :half_width]
    second = value[..., half_width:]
    return jnp.concatenate(
        [first * cosine - second * sine, second * cosine + first * sine], axis=-1
    )


def unrotate(grad_value, cosine, sine):
    half_width = grad_value.shape[-1] // 2
    first = grad_value[..., :half_width]
    second = grad_value[..., half_width:]
    return jnp.concatenate(
        [first * cosine + second * sine, second * cosine - first * sine], axis=-1
    )


def allowed_keys(segment):
    places = jnp.arange(segment.shape[0], dtype=jnp.int32)
    return (segment[:, None] == segment[None, :]) & (places[:, None] >= places[None, :])


def slot_scores(query, key_rows, segment):
    scale = query.shape[-1] ** (-0.5)
    scores = jnp.einsum("qhd,khd->hqk", query, key_rows, preferred_element_type=jnp.float32) * scale
    return jnp.where(allowed_keys(segment)[None], scores, -1e30)


def attend(query, key_rows, value_rows, segment):
    scores = slot_scores(query, key_rows, segment)
    row_max = jnp.max(scores, axis=-1, keepdims=True)
    weights = jnp.exp(scores - row_max)
    total = jnp.sum(weights, axis=-1, keepdims=True)
    probs = (weights / total).astype(jnp.bfloat16)
    attended = jnp.einsum("hqk,khd->qhd", probs, value_rows, preferred_element_type=jnp.float32)
    return (attended.astype(jnp.bfloat16), row_max[..., 0] + jnp.log(total[..., 0]))


def attend_back(query, key_rows, value_rows, segment, logsum, grad_attended):
    scale = query.shape[-1] ** (-0.5)
    scores = slot_scores(query, key_rows, segment)
    probs = jnp.exp(scores - logsum[..., None])
    grad_probs = jnp.einsum(
        "qhd,khd->hqk", grad_attended, value_rows, preferred_element_type=jnp.float32
    )
    delta = jnp.sum(probs * grad_probs, axis=-1, keepdims=True)
    grad_scores = (probs * (grad_probs - delta)).astype(jnp.bfloat16)
    grad_query = (
        jnp.einsum("hqk,khd->qhd", grad_scores, key_rows, preferred_element_type=jnp.float32)
        * scale
    )
    grad_key = (
        jnp.einsum("hqk,qhd->khd", grad_scores, query, preferred_element_type=jnp.float32) * scale
    )
    grad_value = jnp.einsum(
        "hqk,qhd->khd",
        probs.astype(jnp.bfloat16),
        grad_attended,
        preferred_element_type=jnp.float32,
    )
    return (grad_query, grad_key, grad_value)


def gelu_tanh(pre_value):
    return jax.nn.gelu(pre_value, approximate=True)


def local(
    hidden_in,
    earlier,
    gain_attn,
    gain_mlp,
    w_qkv,
    w_out,
    w_up,
    w_down,
    mix_weights,
    lengths,
    slot_perm,
    grad_out,
):
    tensor_count = lax.axis_size("tensor")
    tensor_place = lax.axis_index("tensor")
    own_rows = hidden_in.shape[0]
    model_width = hidden_in.shape[1]
    group_rows = own_rows * tensor_count
    slot_count = lengths.shape[0]
    slot_len = group_rows // slot_count
    own_start = tensor_place * own_rows
    segment, position = slot_layout(lengths, slot_len)
    position = position.reshape(-1)
    back_order = (
        jnp.zeros((group_rows,), jnp.int32)
        .at[slot_perm]
        .set(jnp.arange(group_rows, dtype=jnp.int32))
    )
    cosine, sine = angles(position, HEAD_SIZE)
    gathered_in = lax.all_gather(hidden_in, "tensor", axis=0, tiled=True)
    slot_in = jnp.take(gathered_in, slot_perm, axis=0).astype(jnp.float32)
    normed_attn = layer_norm(slot_in, gain_attn).astype(jnp.bfloat16)
    resid_rows = lax.dynamic_slice_in_dim(slot_in, own_start, own_rows, 0)
    full_qkv, full_out, full_up, full_down = (
        lax.all_gather(w_qkv, "dp", axis=0, tiled=True),
        lax.all_gather(w_out, "dp", axis=1, tiled=True),
        lax.all_gather(w_up, "dp", axis=0, tiled=True),
        lax.all_gather(w_down, "dp", axis=1, tiled=True),
    )
    qkv = jnp.einsum("rd,dcf->rcf", normed_attn, full_qkv, preferred_element_type=jnp.float32)
    heads_dev = qkv.shape[2] // HEAD_SIZE
    shaped = qkv.reshape(group_rows, 3, heads_dev, HEAD_SIZE)
    query = rotate(shaped[:, 0], cosine, sine).astype(jnp.bfloat16)
    key_rows = rotate(shaped[:, 1], cosine, sine).astype(jnp.bfloat16)
    value_rows = shaped[:, 2].astype(jnp.bfloat16)

    def by_slot(value):
        return value.reshape(slot_count, slot_len, heads_dev, HEAD_SIZE)

    attended, logsum = lax.map(
        lambda packed: attend(*packed),
        (by_slot(query), by_slot(key_rows), by_slot(value_rows), segment),
    )
    attn_rows = attended.reshape(group_rows, heads_dev * HEAD_SIZE)
    picked = attn_rows
    after_attn = resid_rows + lax.psum_scatter(
        jnp.dot(picked, full_out, preferred_element_type=jnp.float32),
        "tensor",
        scatter_dimension=0,
        tiled=True,
    )
    normed_mlp = layer_norm(after_attn, gain_mlp).astype(jnp.bfloat16)
    gathered_mlp = lax.all_gather(normed_mlp, "tensor", axis=0, tiled=True)
    pre_act = jnp.dot(gathered_mlp, full_up, preferred_element_type=jnp.float32)
    activated = gelu_tanh(pre_act).astype(jnp.bfloat16)
    placed = lax.dynamic_update_slice_in_dim(
        jnp.zeros((group_rows, model_width), jnp.float32), after_attn, own_start, 0
    )
    picked = back_order
    block_out = lax.psum_scatter(
        jnp.dot(jnp.take(activated, picked, axis=0), full_down, preferred_element_type=jnp.float32)
        + jnp.take(placed, picked, axis=0),
        "tensor",
        scatter_dimension=0,
        tiled=True,
    )
    mixed_total = mix_weights[4] * block_out
    for prior_index in range(4):
        mixed_total = mixed_total + mix_weights[prior_index] * earlier[prior_index].astype(
            jnp.float32
        )
    cotangent = grad_out.astype(jnp.float32)
    grad_earlier = (mix_weights[:4, None, None] * cotangent[None]).astype(jnp.bfloat16)
    mix_terms = [
        jnp.sum(cotangent * earlier[prior_index].astype(jnp.float32)) for prior_index in range(4)
    ]
    mix_grad = jnp.stack(mix_terms + [jnp.sum(cotangent * block_out)])
    gathered_grad = lax.all_gather(grad_out, "tensor", axis=0, tiled=True)
    slot_grad = mix_weights[4] * jnp.take(gathered_grad, slot_perm, axis=0).astype(jnp.float32)
    slot_grad_low = slot_grad.astype(jnp.bfloat16)
    full_qkv, full_out, full_up, full_down = (
        lax.all_gather(w_qkv, "dp", axis=0, tiled=True),
        lax.all_gather(w_out, "dp", axis=1, tiled=True),
        lax.all_gather(w_up, "dp", axis=0, tiled=True),
        lax.all_gather(w_down, "dp", axis=1, tiled=True),
    )
    grad_down = jnp.einsum(
        "rf,rd->fd", activated, slot_grad_low, preferred_element_type=jnp.float32
    )
    grad_act = jnp.einsum("rd,fd->rf", slot_grad_low, full_down, preferred_element_type=jnp.float32)
    unused_value, gelu_back = jax.vjp(gelu_tanh, pre_act)
    grad_pre = gelu_back(grad_act)[0].astype(jnp.bfloat16)
    grad_up = jnp.einsum("rd,rf->df", gathered_mlp, grad_pre, preferred_element_type=jnp.float32)
    picked = grad_pre
    grad_normed_mlp = lax.psum_scatter(
        jnp.einsum("rf,df->rd", picked, full_up, preferred_element_type=jnp.float32),
        "tensor",
        scatter_dimension=0,
        tiled=True,
    )
    unused_norm, second_back = jax.vjp(layer_norm, after_attn, gain_mlp)
    grad_resid_mlp, grad_gain_mlp = second_back(grad_normed_mlp)
    grad_after_attn = lax.dynamic_slice_in_dim(slot_grad, own_start, own_rows, 0) + grad_resid_mlp
    gathered_after = lax.all_gather(
        grad_after_attn.astype(jnp.bfloat16), "tensor", axis=0, tiled=True
    ).astype(grad_after_attn.dtype)
    gathered_low = gathered_after.astype(jnp.bfloat16)
    grad_out_proj = jnp.einsum(
        "rf,rd->fd", attn_rows, gathered_low, preferred_element_type=jnp.float32
    )
    grad_attended = jnp.einsum(
        "rd,fd->rf", gathered_low, full_out, preferred_element_type=jnp.float32
    ).astype(jnp.bfloat16)
    grad_query, grad_key, grad_value = lax.map(
        lambda packed: attend_back(*packed),
        (
            by_slot(query),
            by_slot(key_rows),
            by_slot(value_rows),
            segment,
            logsum,
            by_slot(grad_attended),
        ),
    )
    grad_query = unrotate(grad_query.reshape(group_rows, heads_dev, HEAD_SIZE), cosine, sine)
    grad_key = unrotate(grad_key.reshape(group_rows, heads_dev, HEAD_SIZE), cosine, sine)
    grad_value = grad_value.reshape(group_rows, heads_dev, HEAD_SIZE)
    grad_qkv = (
        jnp.stack([grad_query, grad_key, grad_value], axis=1)
        .reshape(group_rows, 3, heads_dev * HEAD_SIZE)
        .astype(jnp.bfloat16)
    )
    grad_wqkv = jnp.einsum("rd,rcf->dcf", normed_attn, grad_qkv, preferred_element_type=jnp.float32)
    picked = back_order
    grad_normed_attn = lax.psum_scatter(
        jnp.einsum(
            "rcf,dcf->rd",
            jnp.take(grad_qkv, picked, axis=0),
            full_qkv,
            preferred_element_type=jnp.float32,
        ),
        "tensor",
        scatter_dimension=0,
        tiled=True,
    )
    unused_first, first_back = jax.vjp(layer_norm, hidden_in.astype(jnp.float32), gain_attn)
    grad_in_norm, grad_gain_attn = first_back(grad_normed_attn)
    own_order = lax.dynamic_slice_in_dim(back_order, own_start, own_rows, 0)
    carried = jnp.take(gathered_after, own_order, axis=0)
    grad_hidden = (carried + grad_in_norm).astype(jnp.bfloat16)
    send_qkv, send_out, send_up, send_down = (
        lax.psum_scatter(grad_wqkv, "dp", scatter_dimension=0, tiled=True),
        lax.psum_scatter(grad_out_proj, "dp", scatter_dimension=1, tiled=True),
        lax.psum_scatter(grad_up, "dp", scatter_dimension=0, tiled=True),
        lax.psum_scatter(grad_down, "dp", scatter_dimension=1, tiled=True),
    )
    gain_attn_total, gain_mlp_total, mix_total = lax.psum(
        (grad_gain_attn, grad_gain_mlp, mix_grad), ("dp", "tensor")
    )
    return (
        mixed_total.astype(jnp.bfloat16),
        grad_hidden,
        grad_earlier,
        gain_attn_total,
        gain_mlp_total,
        send_qkv,
        send_out,
        send_up,
        send_down,
        mix_total,
    )


def solution(mesh):
    return jax.shard_map(
        local,
        mesh=mesh,
        in_specs=(
            P(("dp", "tensor"), None),
            P(None, ("dp", "tensor"), None),
            P(),
            P(),
            P("dp", None, "tensor"),
            P("tensor", "dp"),
            P("dp", "tensor"),
            P("tensor", "dp"),
            P(),
            P("dp", None),
            P("dp"),
            P(("dp", "tensor"), None),
        ),
        out_specs=(
            P(("dp", "tensor"), None),
            P(("dp", "tensor"), None),
            P(None, ("dp", "tensor"), None),
            P(),
            P(),
            P("dp", None, "tensor"),
            P("tensor", "dp"),
            P("dp", "tensor"),
            P("tensor", "dp"),
            P(),
        ),
        check_vma=False,
    )
```

profile of v0, /device:TPU:0, one launch (start us, length us, event | category | flops | bytes accessed | tf_op | source)
XLA Modules:
  0.0 926.1 jit_solution(7272461658670504872)
XLA Ops:
  13.2 38.5 %all_gather.29 = bf16[768,3,192]{2,1,0:T(4,128)(2,1)S(1)} all-gather(bf16[96,3,192]{2,1,0:T(4,128)(2,1)S(1)} %copy.77), channel_id=1, replica_groups=mesh['dp'=8,'tensor'=4] {'dp'}, dimensions={0}, use_global_device_ids=true | all-gather | bytes 995328 | tf_op jit(solution)/shard_map/all_gather | solution.py:139
  53.9 17.5 %gather_fusion.3 = s32[2048]{0:T(1024)S(1)} fusion(s32[2,5]{1,0:T(2,128)S(1)} %pad_add_fusion, s32[2048]{0:T(1024)S(1)} %bitcast.212), kind=kCustom, calls=%fused_computation.6 | custom fusion | bytes 32768 | tf_op jit(solution)/shard_map/jit(take_along_axis)/gather | solution.py:25
  72.1 33.1 %all_gather.30 = bf16[192,768]{0,1:T(8,128)(2,1)} all-gather(bf16[192,96]{0,1:T(8,128)(2,1)S(1)} %copy.83), channel_id=1, replica_groups=mesh['dp'=8,'tensor'=4] {'dp'}, dimensions={1}, use_global_device_ids=true | all-gather | bytes 331776 | tf_op jit(solution)/shard_map/all_gather | solution.py:140
  107.6 10.8 %gather_fusion.4 = bf16[2048,768]{1,0:T(8,128)(2,1)S(1)} fusion(bf16[2048,768]{1,0:T(8,128)(2,1)} %all-gather.7.cloned.1.call-done, s32[2048]{0:T(1024)S(1)} %get-tuple-element.246), kind=kCustom, calls=%fused_computation.clone | custom fusion | bytes 6299648 | tf_op jit(solution)/shard_map/jit(_take)/gather | solution.py:135
  119.6 12.4 %gather_fusion.6 = bf16[2048,768]{1,0:T(8,128)(2,1)} fusion(bf16[2048,768]{1,0:T(8,128)(2,1)} %all-gather.15.cloned.1.call-done, s32[2048]{0:T(1024)S(1)} %get-tuple-element.246), kind=kCustom, calls=%fused_computation.2.clone | custom fusion | bytes 6299648 | tf_op jit(solution)/shard_map/jit(_take)/gather | solution.py:193
  149.0 30.5 %while.26 = (s32[]{:T(128)}, bf16[2,1024,3,64]{1,3,2,0:T(8,128)(2,1)}, f32[2,3,1024]{2,1,0:T(4,128)}, bf16[2,1024,3,64]{1,3,2,0:T(8,128)(2,1)}, s32[2,1024]{1,0:...) while((s32[]{:T(128)}, ...), condition=%wide.region_7.9_spmd, body=%wide.region_4.8_spmd.sunk | while | flops 846394368 | bytes 47827072 | solution.py:154
  191.1 53.4 %reduce-scatter.11.cloned.1.call-done = f32[512,768]{1,0:T(8,128)} async-done(((f32[2048,768]{1,0:T(8,128)}), f32[512,768]{1,0:T(8,128)}) %reduce-scatter.11.cloned.1.call-update) | async-done | bytes 1572880 | tf_op jit(solution)/shard_map/reduce_scatter | solution.py:160
  250.2 27.8 %all-gather.9.cloned.1.call-done = bf16[2048,768]{1,0:T(8,128)(2,1)} async-done(((bf16[512,768]{1,0:T(8,128)(2,1)}), bf16[2048,768]{1,0:T(8,128)(2,1)}) %all-gather.9.cloned.1.call-update) | async-done | bytes 3145744 | tf_op jit(solution)/shard_map/all_gather | solution.py:167
  278.0 8.5 multiply_convert_fusion.2
  286.5 35.0 %all-gather.13.cloned.1.call-done = bf16[768,768]{0,1:T(8,128)(2,1)} async-done(((bf16[768,96]{0,1:T(8,128)(2,1)}), bf16[768,768]{0,1:T(8,128)(2,1)}) %all-gather.13.cloned.1.call-update) | async-done | bytes 1179664 | tf_op jit(solution)/shard_map/all_gather | solution.py:142
  321.5 9.7 %fusion.60 = bf16[2048,768]{1,0:T(8,128)(2,1)S(1)} fusion(f32[2048,768]{1,0:T(8,128)} %get-tuple-element.257, bf16[768,768]{0,1:T(8,128)(2,1)} %all-gather.13.cloned.1.call-done, bf16[2048,768]{1,0:T(8,128)(2,1)} %gather_fusion.6, f32[]{:T(128)} %bitcast.19, pred[2048]{0:T(1024)(128)(4,1)} %copy-done.39), kind=kOutput, calls=%fused_computation.79 | convolution fusion | flops 2453667840 | bytes 13764612 | tf_op jit(solution)/shard_map/rd,fd->rf/dot_general | solution.py:204
  337.6 57.2 %reduce-scatter.15.cloned.1.call-done = f32[512,768]{1,0:T(8,128)} async-done(((f32[2048,768]{1,0:T(8,128)}), f32[512,768]{1,0:T(8,128)}) %reduce-scatter.15.cloned.1.call-update) | async-done | bytes 1572880 | tf_op jit(solution)/shard_map/reduce_scatter | solution.py:209
  406.8 8.2 scatter_custom_fusion
  415.0 19.6 %all-gather.17.cloned.1.call-done = bf16[2048,768]{1,0:T(8,128)(2,1)} async-done(((bf16[512,768]{1,0:T(8,128)(2,1)}), bf16[2048,768]{1,0:T(8,128)(2,1)}) %all-gather.17.cloned.1.call-update) | async-done | bytes 3145744 | tf_op jit(solution)/shard_map/all_gather | solution.py:218
  440.3 9.5 %gather_fusion.5 = bf16[2048,768]{1,0:T(8,128)(2,1)} fusion(bf16[2048,768]{1,0:T(8,128)(2,1)S(1)} %get-tuple-element.256, s32[2048]{0:T(1024)S(1)} %fusion.96), kind=kCustom, calls=%fused_computation.1.clone | custom fusion | bytes 6299648 | tf_op jit(solution)/shard_map/jit(_take)/gather | solution.py:175
  449.8 13.6 %gather_fusion = f32[2048,768]{1,0:T(8,128)} fusion(f32[2048,768]{1,0:T(8,128)} %get-tuple-element.238, s32[2048]{0:T(1024)S(1)} %fusion.96), kind=kCustom, calls=%fused_computation.3 | custom fusion | bytes 12591104 | tf_op jit(solution)/shard_map/jit(_take)/gather | solution.py:176
  476.2 114.8 %while.27 = (s32[]{:T(128)}, f32[2,1024,3,64]{1,0,3,2:T(2,128)}, f32[2,1024,3,64]{1,0,3,2:T(2,128)}, bf16[2,1024,3,64]{1,3,2,0:T(8,128)(2,1)}, bf16[2,1024,3,64]...) while((s32[]{:T(128)}, f32[2,1024,3,64]{1,0,3,2:T(2,128)}, ...), condition=%wide.region_18.20_spmd, body=%wide.region_16.19_spmd.sunk | while | flops 2063987712 | bytes 116366528 | solution.py:228
  484.3 8.6 multiply_reduce_fusion.6
  504.8 14.4 %dynamic_update_slice.35 = f32[2,1024,3,64]{1,0,3,2:T(2,128)} dynamic-update-slice(f32[2,1024,3,64]{1,0,3,2:T(2,128)} %get-tuple-element.410, f32[1,1024,3,64]{1,0,3,2:T(1,128)S(1)} %copy.139, s32[]{:T(128)S(6)} %copy.159, s32[]{:T(128)} %constant.115.clone.1..sunk, s32[]{:T(128)} %constant.115.clone.1..sunk, s32[]{:T(128)} %constant.115.clone.1..sunk) | dynamic-update-slice | bytes 1572868 | tf_op jit(solution)/shard_map/while/body/jit(dynamic_update_index_in_dim)/dynamic_update_slice | solution.py:228
  519.2 14.3 %dynamic_update_slice.34 = f32[2,1024,3,64]{1,0,3,2:T(2,128)} dynamic-update-slice(f32[2,1024,3,64]{1,0,3,2:T(2,128)} %get-tuple-element.409, f32[1,1024,3,64]{1,0,3,2:T(1,128)S(1)} %copy.138, s32[]{:T(128)S(6)} %copy.159, s32[]{:T(128)} %constant.115.clone.1..sunk, s32[]{:T(128)} %constant.115.clone.1..sunk, s32[]{:T(128)} %constant.115.clone.1..sunk) | dynamic-update-slice | bytes 1572868 | tf_op jit(solution)/shard_map/while/body/jit(dynamic_update_index_in_dim)/dynamic_update_slice | solution.py:228
  541.4 8.6 multiply_reduce_fusion.6
  562.0 14.3 %dynamic_update_slice.35 = f32[2,1024,3,64]{1,0,3,2:T(2,128)} dynamic-update-slice(f32[2,1024,3,64]{1,0,3,2:T(2,128)} %get-tuple-element.410, f32[1,1024,3,64]{1,0,3,2:T(1,128)S(1)} %copy.139, s32[]{:T(128)S(6)} %copy.159, s32[]{:T(128)} %constant.115.clone.1..sunk, s32[]{:T(128)} %constant.115.clone.1..sunk, s32[]{:T(128)} %constant.115.clone.1..sunk) | dynamic-update-slice | bytes 1572868 | tf_op jit(solution)/shard_map/while/body/jit(dynamic_update_index_in_dim)/dynamic_update_slice | solution.py:228
  576.3 14.3 %dynamic_update_slice.34 = f32[2,1024,3,64]{1,0,3,2:T(2,128)} dynamic-update-slice(f32[2,1024,3,64]{1,0,3,2:T(2,128)} %get-tuple-element.409, f32[1,1024,3,64]{1,0,3,2:T(1,128)S(1)} %copy.138, s32[]{:T(128)S(6)} %copy.159, s32[]{:T(128)} %constant.115.clone.1..sunk, s32[]{:T(128)} %constant.115.clone.1..sunk, s32[]{:T(128)} %constant.115.clone.1..sunk) | dynamic-update-slice | bytes 1572868 | tf_op jit(solution)/shard_map/while/body/jit(dynamic_update_index_in_dim)/dynamic_update_slice | solution.py:228
  606.3 18.7 %gather_fusion.2 = bf16[2048,3,192]{2,1,0:T(4,128)(2,1)} fusion(bf16[2048,3,192]{2,1,0:T(4,128)(2,1)} %copy.91, s32[2048]{0:T(1024)S(1)} %copy-done.29), kind=kCustom, calls=%fused_computation.5 | custom fusion | bytes 4726784 | tf_op jit(solution)/shard_map/jit(_take)/gather | solution.py:252
  625.1 9.7 %broadcast_select_fusion = bf16[2048,3,192]{2,1,0:T(4,128)(2,1)S(1)} fusion(bf16[2048,3,192]{2,1,0:T(4,128)(2,1)} %gather_fusion.2, pred[2048]{0:T(1024)(128)(4,1)S(1)} %copy-done.45), kind=kLoop, calls=%fused_computation.87 | loop fusion | flops 1179648 | bytes 4720640 | tf_op jit(solution)/shard_map/jit(_take)/select_n | solution.py:252
  647.1 8.0 fusion.85
  677.6 8.4 fusion.83
  689.3 9.2 reduce-scatter.17.cloned.1.call-done
  701.4 40.5 %all-reduce = (f32[768]{0:T(1024)}, f32[768]{0:T(1024)}, f32[5]{0:T(128)}) all-reduce(f32[768]{0:T(1024)S(1)} %get-tuple-element.175, f32[768]{0:T(1024)S(1)} %copy-done.44, f32[5]{0:T(128)S(1)} %stack.38), channel_id=1, replica_groups=mesh['dp'=8,'tensor'=4] {'dp','tensor'}, use_global_device_ids=true, to_apply=%region_25.27 | all-reduce | flops 1541 | bytes 12328 | tf_op jit(solution)/shard_map/psum | solution.py:271
  744.8 27.5 %reduce-scatter.21.cloned.1.call-done = f32[96,768]{1,0:T(8,128)} async-done(((f32[768,768]{1,0:T(8,128)}), f32[96,768]{1,0:T(8,128)}) %reduce-scatter.21.cloned.1.call-update) | async-done | bytes 294928 | tf_op jit(solution)/shard_map/reduce_scatter | solution.py:268
  772.4 73.1 %reduce-scatter.23.cloned.1.call-done = f32[768,96]{0,1:T(8,128)} async-done(((f32[768,768]{0,1:T(8,128)}), f32[768,96]{0,1:T(8,128)}) %reduce-scatter.23.cloned.1.call-update) | async-done | bytes 294928 | tf_op jit(solution)/shard_map/reduce_scatter | solution.py:269
  845.4 73.1 %reduce-scatter.19.cloned.1.call-done = f32[96,3,192]{2,0,1:T(8,128)} async-done(((f32[768,3,192]{2,0,1:T(8,128)}), f32[96,3,192]{2,0,1:T(8,128)}) %reduce-scatter.19.cloned.1.call-update) | async-done | bytes 221200 | tf_op jit(solution)/shard_map/reduce_scatter | solution.py:266
  (261 shorter events, 211.0 us)
Async XLA Ops:
  8.0 99.6 %all-gather.7.cloned.1.call-start = ((), (), s32[]{:S(2)}) async-start(), calls=%async_computation.8 | async-start | bytes 3932160 | tf_op jit(solution)/shard_map/all_gather | solution.py:134
  8.7 110.8 %all-gather.15.cloned.1.call-start = ((), (), s32[]{:S(2)}) async-start(), calls=%async_computation.14 | async-start | bytes 3932160 | tf_op jit(solution)/shard_map/all_gather | solution.py:192
  9.5 235.0 %reduce-scatter.11.cloned.1.call-start = ((), (), s32[]{:S(2)}) async-start(), calls=%async_computation.9 | async-start | bytes 7864320 | tf_op jit(solution)/shard_map/reduce_scatter | solution.py:160
  53.9 17.6 %copy-start.42 = (f32[5]{0:T(128)S(1)}, f32[5]{0:T(128)}, u32[]{:S(2)}) copy-start(f32[5]{0:T(128)} %param.26) | copy-start | bytes 64
  53.9 51.3 %copy-start.34 = (s32[2048]{0:T(1024)S(1)}, s32[2048]{0:T(1024)}, u32[]{:S(2)}) copy-start(s32[2048]{0:T(1024)} %param.28) | copy-start | bytes 24580
  105.2 81.7 %copy-start.39 = (pred[2048]{0:T(1024)(128)(4,1)}, pred[2048]{0:T(1024)(128)(4,1)S(1)}, u32[]{:S(2)}) copy-start(pred[2048]{0:T(1024)(128)(4,1)S(1)} %compare_and_fusion.1) | copy-start | bytes 6148
  107.6 33.3 %copy-start.20 = (f32[2048,32]{0,1:T(8,128)}, f32[2048,32]{0,1:T(8,128)S(1)}, u32[]{:S(2)}) copy-start(f32[2048,32]{0,1:T(8,128)S(1)} %get-tuple-element.243) | copy-start | bytes 786436
  118.4 19.4 %copy-start.3 = (bf16[2048,768]{1,0:T(8,128)(2,1)}, bf16[2048,768]{1,0:T(8,128)(2,1)S(1)}, u32[]{:S(2)}) copy-start(bf16[2048,768]{1,0:T(8,128)(2,1)S(1)} %gather_fusion.4) | copy-start | bytes 9437188
  119.5 18.4 %copy-start.37 = (f32[2048]{0:T(1024)}, f32[2048]{0:T(1024)S(1)}, u32[]{:S(2)}) copy-start(f32[2048]{0:T(1024)S(1)} %broadcast_multiply_fusion) | copy-start | bytes 24580
  186.3 63.9 %all-gather.11.cloned.1.call-start = ((), (), s32[]{:S(2)}) async-start(), calls=%async_computation.11 | async-start | bytes 1327104 | tf_op jit(solution)/shard_map/all_gather | solution.py:141
  186.9 91.1 %all-gather.9.cloned.1.call-start = ((), (), s32[]{:S(2)}) async-start(), calls=%async_computation.10 | async-start | bytes 3932160 | tf_op jit(solution)/shard_map/all_gather | solution.py:167
  191.1 57.3 %copy-start.31 = (f32[768]{0:T(1024)S(1)}, f32[768]{0:T(1024)}, u32[]{:S(2)}) copy-start(f32[768]{0:T(1024)} %param.21) | copy-start | bytes 9220
  249.5 72.0 %all-gather.13.cloned.1.call-start = ((), (), s32[]{:S(2)}) async-start(), calls=%async_computation.12 | async-start | bytes 1327104 | tf_op jit(solution)/shard_map/all_gather | solution.py:142
  250.1 144.7 %reduce-scatter.15.cloned.1.call-start = ((), (), s32[]{:S(2)}) async-start(), calls=%async_computation.15 | async-start | bytes 7864320 | tf_op jit(solution)/shard_map/reduce_scatter | solution.py:209
  286.5 153.8 %copy-start = (bf16[2048,768]{1,0:T(8,128)(2,1)}, bf16[2048,768]{1,0:T(8,128)(2,1)S(1)}, u32[]{:S(2)}) copy-start(bf16[2048,768]{1,0:T(8,128)(2,1)S(1)} %get-tuple-element.256) | copy-start | bytes 9437188
  321.5 11.5 %copy-start.48 = (bf16[768,768]{1,0:T(8,128)(2,1)S(1)}, bf16[768,768]{1,0:T(8,128)(2,1)}, u32[]{:S(2)}) copy-start(bf16[768,768]{1,0:T(8,128)(2,1)} %all-gather.11.cloned.1.call-done) | copy-start | bytes 3538948
  337.6 97.0 %all-gather.17.cloned.1.call-start = ((), (), s32[]{:S(2)}) async-start(), calls=%async_computation.16 | async-start | bytes 3932160 | tf_op jit(solution)/shard_map/all_gather | solution.py:218
  406.1 269.9 %reduce-scatter.25.cloned.1.call-start = ((), (), s32[]{:S(2)}) async-start(), calls=%async_computation.21 | async-start | bytes 884736
  414.9 24.0 %copy-start.30 = (s32[2048]{0:T(1024)}, s32[2048]{0:T(1024)S(1)}, u32[]{:S(2)}) copy-start(s32[2048]{0:T(1024)S(1)} %scatter_custom_fusion) | copy-start | bytes 24580
  438.9 238.7 %reduce-scatter.13.cloned.1.call-start = ((), (), s32[]{:S(2)}) async-start(), calls=%async_computation.13 | async-start | bytes 7864320 | tf_op jit(solution)/shard_map/reduce_scatter | solution.py:174
  440.3 9.5 %copy-start.28 = (s32[2048]{0:T(1024)}, s32[2048]{0:T(1024)S(1)}, u32[]{:S(2)}) copy-start(s32[2048]{0:T(1024)S(1)} %fusion.96) | copy-start | bytes 24580
  449.8 13.6 %copy-start.19 = (bf16[2048,768]{1,0:T(8,128)(2,1)S(1)}, bf16[2048,768]{1,0:T(8,128)(2,1)}, u32[]{:S(2)}) copy-start(bf16[2048,768]{1,0:T(8,128)(2,1)} %gather_fusion.5) | copy-start | bytes 9437188
  471.3 227.3 %reduce-scatter.17.cloned.1.call-start = ((), (), s32[]{:S(2)}) async-start(), calls=%async_computation.17 | async-start | bytes 7864320 | tf_op jit(solution)/shard_map/reduce_scatter | solution.py:249
  484.3 8.6 copy-start.27
  541.4 8.6 copy-start.27
  606.3 18.7 %copy-start.45 = (pred[2048]{0:T(1024)(128)(4,1)S(1)}, pred[2048]{0:T(1024)(128)(4,1)}, u32[]{:S(2)}) copy-start(pred[2048]{0:T(1024)(128)(4,1)} %compare_and_fusion) | copy-start | bytes 6148
  625.1 9.7 %copy-start.25 = (bf16[768,3,192]{0,2,1:T(8,128)(2,1)S(1)}, bf16[768,3,192]{0,2,1:T(8,128)(2,1)}, u32[]{:S(2)}) copy-start(bf16[768,3,192]{0,2,1:T(8,128)(2,1)} %copy.78) | copy-start | bytes 2654212
  639.6 132.7 %reduce-scatter.21.cloned.1.call-start = ((), (), s32[]{:S(2)}) async-start(), calls=%async_computation.19 | async-start | bytes 2654208 | tf_op jit(solution)/shard_map/reduce_scatter | solution.py:268
  646.8 8.4 copy-start.33
  646.9 198.6 %reduce-scatter.23.cloned.1.call-start = ((), (), s32[]{:S(2)}) async-start(), calls=%async_computation.20 | async-start | bytes 2654208 | tf_op jit(solution)/shard_map/reduce_scatter | solution.py:269
  655.2 263.4 %reduce-scatter.19.cloned.1.call-start = ((), (), s32[]{:S(2)}) async-start(), calls=%async_computation.18 | async-start | bytes 2654208 | tf_op jit(solution)/shard_map/reduce_scatter | solution.py:266
  686.0 15.4 %copy-start.44 = (f32[768]{0:T(1024)S(1)}, f32[768]{0:T(1024)}, u32[]{:S(2)}) copy-start(f32[768]{0:T(1024)} %get-tuple-element.173) | copy-start | bytes 9220
  (35 other events, 122.0 us)
Sparse Core Ops, SparseCore 0:
  10.4 31.2 all-gather.6
  43.2 28.4 all-gather.14
  186.4 58.0 reduce-scatter.10
Sparse Core Ops, SparseCore 1:
  189.0 40.6 all-gather.10
  249.6 28.3 all-gather.8
  280.1 41.4 all-gather.12
  337.7 57.1 reduce-scatter.14
  406.2 28.3 all-gather.16
  439.0 63.3 reduce-scatter.24
  504.8 57.7 reduce-scatter.12
  639.7 58.8 reduce-scatter.16
  702.5 69.8 reduce-scatter.20
  776.5 68.9 reduce-scatter.22
  849.4 69.1 reduce-scatter.18
where the time goes:
time: 941 us; the launch traced here: 926 us
  waiting for transfers between devices  379 us (40%)
  local copies, waits for them, and re-layouts  201 us (21%)
  matrix products  129 us (14%)
  blocking collectives  112 us (12%)
  other arithmetic  87.5 us (9%)
  between operations  16.5 us (2%)
    reduce_scatter x1, waiting for transfers between devices, local(): lax.psum_scatter(grad_wqkv, 'dp', scatter_dimension=0, tiled=True)  73.1 us
    reduce_scatter x1, waiting for transfers between devices, local(): lax.psum_scatter(grad_down, 'dp', scatter_dimension=1, tiled=True)  73.1 us
    dynamic_update_slice x8, local copies, waits for them, and re-layouts, local(): lax.map(lambda packed: attend_back(*packed), (by_slot(query), by_slot(key...  60.5 us
    reduce_scatter x1, waiting for transfers between devices, local(): lax.psum_scatter(jnp.einsum('rf,df->rd', picked, full_up, preferred_eleme...  57.2 us
    reduce_scatter x1, waiting for transfers between devices, local(): lax.psum_scatter(jnp.dot(picked, full_out, preferred_element_type=jnp.flo...  53.4 us
    psum x1, blocking collectives, local(): lax.psum((grad_gain_attn, grad_gain_mlp, mix_grad), ('dp', 'tensor'))  40.5 us
    all_gather x1, blocking collectives, local(): lax.all_gather(w_qkv, 'dp', axis=0, tiled=True)  38.5 us
    all_gather x1, waiting for transfers between devices, local(): lax.all_gather(w_down, 'dp', axis=1, tiled=True)  35 us
  transfers between devices with their start and end apart: 14, of which 9 were waited for; matrix products, arithmetic and copies ran while one was open for 34% of the time, Pallas kernels for 0%

commit v1 on v0

v1 whole, which is shorter than its diff:
```python
import jax
import jax.numpy as jnp
from jax import lax
from jax.experimental import pallas as pl
from jax.experimental.pallas import tpu as pltpu
from jax.sharding import PartitionSpec as P

HEAD_SIZE = 64
HALF = HEAD_SIZE // 2
LANES = 128
LOG2E = 1.4426950408889634
ROW_STEP = 256

eps = 1e-05
bf16 = jnp.bfloat16
f32 = jnp.float32


def layer_norm(value, gain):
    row_mean = jnp.mean(value, axis=-1, keepdims=True)
    centered = value - row_mean
    spread = jnp.mean(centered * centered, axis=-1, keepdims=True)
    return centered * lax.rsqrt(spread + eps) * gain


def slot_layout(lengths, slot_len):
    ends = jnp.cumsum(lengths, axis=-1)
    places = jnp.arange(slot_len, dtype=jnp.int32)
    passed = places[None, :, None] >= ends[:, None, :]
    first = jnp.max(jnp.where(passed, ends[:, None, :], 0), axis=-1)
    return (first, places[None, :] - first)


def angle_tables(position):
    inverse = 1.0 / 10000.0 ** (jnp.arange(HALF, dtype=f32) * (2.0 / HEAD_SIZE))
    phase_angle = position.astype(f32)[:, None] * inverse[None, :]
    cosine = jnp.cos(phase_angle)
    sine = jnp.sin(phase_angle)
    repeat = LANES // HEAD_SIZE
    return (
        jnp.concatenate([cosine, cosine] * repeat, axis=1),
        jnp.concatenate([-sine, sine] * repeat, axis=1),
    )


def swap_halves(value):
    lane = lax.broadcasted_iota(jnp.int32, value.shape, 1)
    low = (lane % HEAD_SIZE) < HALF
    return jnp.where(low, pltpu.roll(value, LANES - HALF, 1), pltpu.roll(value, HALF, 1))


def turn(value, cosine, sine):
    return value * cosine + swap_halves(value) * sine


def dot(a, b, dims=((1,), (0,))):
    return lax.dot_general(a, b, (dims, ((), ())), preferred_element_type=f32)


def project_kernel(n0, n1, n2, n3, perm_ref, w_ref, cos_ref, sin_ref, slot_ref, qkv_ref):
    pieces = (n0, n1, n2, n3)
    rows = perm_ref.shape[0]
    each = n0.shape[0]
    wanted = perm_ref[...]
    total = None
    for k in range(4):
        here = lax.broadcasted_iota(jnp.int32, (rows, each), 1) + k * each
        pick = jnp.where(here == wanted, 1.0, 0.0).astype(bf16)
        part = dot(pick, pieces[k][...])
        total = part if total is None else total + part
    normed = total.astype(bf16)
    slot_ref[...] = normed
    qkv = dot(normed, w_ref[...])
    cosine = cos_ref[...]
    sine = sin_ref[...]
    third = qkv.shape[1] // 3
    for start in range(0, 2 * third, LANES):
        qkv_ref[:, start : start + LANES] = turn(
            qkv[:, start : start + LANES], cosine, sine
        ).astype(bf16)
    qkv_ref[:, 2 * third :] = qkv[:, 2 * third :].astype(bf16)


def project(pieces, perm_col, w, cosine, sine):
    each, width = pieces[0].shape
    rows = perm_col.shape[0]
    cols = w.shape[1]
    whole = pl.BlockSpec((each, width), lambda i: (0, 0))
    return pl.pallas_call(
        project_kernel,
        grid=(rows // ROW_STEP,),
        in_specs=[whole] * 4
        + [
            pl.BlockSpec((ROW_STEP, 1), lambda i: (i, 0)),
            pl.BlockSpec(w.shape, lambda i: (0, 0)),
            pl.BlockSpec((ROW_STEP, LANES), lambda i: (i, 0)),
            pl.BlockSpec((ROW_STEP, LANES), lambda i: (i, 0)),
        ],
        out_specs=[
            pl.BlockSpec((ROW_STEP, width), lambda i: (i, 0)),
            pl.BlockSpec((ROW_STEP, cols), lambda i: (i, 0)),
        ],
        out_shape=[
            jax.ShapeDtypeStruct((rows, width), bf16),
            jax.ShapeDtypeStruct((rows, cols), bf16),
        ],
        name="project",
    )(*pieces, perm_col, w, cosine, sine)


def spread_rows(perm_ref, value, start, count):
    total = value.shape[0]
    here = lax.broadcasted_iota(jnp.int32, (count, total), 0) + start
    pick = jnp.where(here == perm_ref[...], 1.0, 0.0).astype(bf16)
    return dot(pick, value)


def masked(scores, first_row, query_start):
    key = lax.broadcasted_iota(jnp.int32, scores.shape, 0)
    query = lax.broadcasted_iota(jnp.int32, scores.shape, 1) + query_start
    return jnp.where((key >= first_row) & (key <= query), scores, -1e30)


def attend_kernel(qkv_ref, first_ref, perm_ref, o0, o1, o2, o3, stat_ref, o_all):
    slot = pl.program_id(0)
    length, cols = qkv_ref.shape
    third = cols // 3
    factor = HEAD_SIZE ** (-0.5) * LOG2E
    for head in range(third // HEAD_SIZE):
        at = head * HEAD_SIZE
        key = qkv_ref[:, third + at : third + at + HEAD_SIZE]
        value = qkv_ref[:, 2 * third + at : 2 * third + at + HEAD_SIZE]
        value_t = value.T
        for start in range(0, length, ROW_STEP):
            seen = start + ROW_STEP
            query = qkv_ref[start:seen, at : at + HEAD_SIZE]
            scores = dot(key[:seen], query, ((1,), (1,)))
            scores = masked(scores, first_ref[0, :, start:seen], start)
            top = jnp.max(scores, axis=0, keepdims=True)
            weights = jnp.exp2((scores - top) * factor)
            mass = jnp.sum(weights, axis=0, keepdims=True)
            probs = (weights * (1.0 / mass)).astype(bf16)
            out = dot(value_t[:, :seen], probs).T
            stat_ref[0, head : head + 1, start:seen] = top * factor + jnp.log2(mass)
            o_all[pl.ds(slot * length + start, ROW_STEP), at : at + HEAD_SIZE] = out.astype(bf16)

    @pl.when(slot == pl.num_programs(0) - 1)
    def _():
        each = o0.shape[0]
        for k, ref in enumerate((o0, o1, o2, o3)):
            ref[...] = spread_rows(perm_ref, o_all[...], k * each, each).astype(bf16)


def attend(qkv, first, perm_row, each):
    slots, _, length = first.shape
    rows, cols = qkv.shape
    third = cols // 3
    piece = pl.BlockSpec((each, third), lambda i: (0, 0))
    return pl.pallas_call(
        attend_kernel,
        grid=(slots,),
        in_specs=[
            pl.BlockSpec((length, cols), lambda i: (i, 0)),
            pl.BlockSpec((1, 1, length), lambda i: (i, 0, 0)),
            pl.BlockSpec((1, rows), lambda i: (0, 0)),
        ],
        out_specs=[piece] * 4 + [pl.BlockSpec((1, 8, length), lambda i: (i, 0, 0))],
        out_shape=[jax.ShapeDtypeStruct((each, third), bf16)] * 4
        + [jax.ShapeDtypeStruct((slots, 8, length), f32)],
        scratch_shapes=[pltpu.VMEM((rows, third), bf16)],
        name="attend",
    )(qkv, first, perm_row)


def attend_back_kernel(
    qkv_ref, first_ref, perm_ref, d0, d1, d2, d3, stat_ref, cos_ref, sin_ref, out_ref, acc, given
):
    length, cols = qkv_ref.shape
    third = cols // 3
    scale = HEAD_SIZE ** (-0.5)
    factor = scale * LOG2E
    each = d0.shape[0]
    for start in range(0, length, ROW_STEP):
        total = None
        for k, ref in enumerate((d0, d1, d2, d3)):
            here = lax.broadcasted_iota(jnp.int32, (ROW_STEP, each), 1) + k * each
            pick = jnp.where(here == perm_ref[start : start + ROW_STEP, :], 1.0, 0.0).astype(bf16)
            part = dot(pick, ref[...])
            total = part if total is None else total + part
        given[start : start + ROW_STEP, :] = total.astype(bf16)
    acc[:, third:] = jnp.zeros((length, 2 * third), f32)
    for head in range(third // HEAD_SIZE):
        at = head * HEAD_SIZE
        key = qkv_ref[:, third + at : third + at + HEAD_SIZE]
        value = qkv_ref[:, 2 * third + at : 2 * third + at + HEAD_SIZE]
        key_t = key.T
        for start in range(0, length, ROW_STEP):
            seen = start + ROW_STEP
            query = qkv_ref[start:seen, at : at + HEAD_SIZE]
            grad = given[start:seen, at : at + HEAD_SIZE]
            scores = dot(key[:seen], query, ((1,), (1,)))
            scores = masked(scores, first_ref[0, :, start:seen], start)
            probs = jnp.exp2(scores * factor - stat_ref[0, head : head + 1, start:seen])
            grad_probs = dot(value[:seen], grad, ((1,), (1,)))
            delta = jnp.sum(probs * grad_probs, axis=0, keepdims=True)
            grad_scores = (probs * (grad_probs - delta)).astype(bf16)
            acc[start:seen, at : at + HEAD_SIZE] = dot(key_t[:, :seen], grad_scores).T
            acc[:seen, third + at : third + at + HEAD_SIZE] += dot(grad_scores, query)
            acc[:seen, 2 * third + at : 2 * third + at + HEAD_SIZE] += dot(
                probs.astype(bf16), grad
            )
    cosine = cos_ref[...]
    sine = -sin_ref[...]
    for start in range(0, 2 * third, LANES):
        out_ref[:, start : start + LANES] = turn(
            acc[:, start : start + LANES] * scale, cosine, sine
        ).astype(bf16)
    out_ref[:, 2 * third :] = acc[:, 2 * third :].astype(bf16)


def attend_back(qkv, first, perm_col, grads, stat, cosine, sine):
    slots, _, length = first.shape
    rows, cols = qkv.shape
    third = cols // 3
    piece = pl.BlockSpec(grads[0].shape, lambda i: (0, 0))
    return pl.pallas_call(
        attend_back_kernel,
        grid=(slots,),
        in_specs=[
            pl.BlockSpec((length, cols), lambda i: (i, 0)),
            pl.BlockSpec((1, 1, length), lambda i: (i, 0, 0)),
            pl.BlockSpec((length, 1), lambda i: (i, 0)),
        ]
        + [piece] * 4
        + [
            pl.BlockSpec((1, 8, length), lambda i: (i, 0, 0)),
            pl.BlockSpec((length, LANES), lambda i: (i, 0)),
            pl.BlockSpec((length, LANES), lambda i: (i, 0)),
        ],
        out_specs=pl.BlockSpec((length, cols), lambda i: (i, 0)),
        out_shape=jax.ShapeDtypeStruct((rows, cols), bf16),
        scratch_shapes=[pltpu.VMEM((length, cols), f32), pltpu.VMEM((length, third), bf16)],
        name="attend_back",
    )(qkv, first, perm_col, *grads, stat, cosine, sine)


def unproject(dqkv, perm_row, w, each):
    rows, cols = dqkv.shape
    width = w.shape[0]

    def kernel(dqkv_ref, perm_ref, w_ref, out_ref):
        start = pl.program_id(0) * ROW_STEP
        picked = spread_rows(perm_ref, dqkv_ref[...], start, ROW_STEP).astype(bf16)
        out_ref[...] = dot(picked, w_ref[...], ((1,), (1,))).astype(bf16)

    return pl.pallas_call(
        kernel,
        grid=(rows // ROW_STEP,),
        in_specs=[
            pl.BlockSpec((rows, cols), lambda i: (0, 0)),
            pl.BlockSpec((1, rows), lambda i: (0, 0)),
            pl.BlockSpec(w.shape, lambda i: (0, 0)),
        ],
        out_specs=pl.BlockSpec((ROW_STEP, width), lambda i: (i, 0)),
        out_shape=jax.ShapeDtypeStruct((rows, width), bf16),
        name="unproject",
    )(dqkv, perm_row, w)


def hop(value, axis, bit):
    count = lax.axis_size(axis)
    return lax.ppermute(value, axis, [(i, i ^ bit) for i in range(count)])


def gather_tensor(value):
    far = hop(value, "tensor", 2)
    near = hop(value, "tensor", 1)
    cross = hop(far, "tensor", 1)
    return [value, near, far, cross]


def exchange_tensor(pieces):
    return [pieces[0]] + [hop(pieces[k], "tensor", k) for k in (1, 2, 3)]


def scatter_tensor(pieces):
    over = hop(pieces[3].astype(bf16), "tensor", 1)
    beside = hop(pieces[1].astype(bf16), "tensor", 1)
    outward = (pieces[2].astype(f32) + over.astype(f32)).astype(bf16)
    back = hop(outward, "tensor", 2)
    return pieces[0].astype(f32) + beside.astype(f32) + back.astype(f32)


def total_all(value):
    for axis in ("tensor", "dp"):
        bit = 1
        while bit < lax.axis_size(axis):
            value = value + hop(value, axis, bit)
            bit *= 2
    return value


def gather_dp(value):
    return lax.all_gather(value, "dp", axis=0, tiled=True)


def scatter_dp(value):
    return lax.psum_scatter(value.astype(bf16), "dp", scatter_dimension=0, tiled=True).astype(f32)


def gelu_tanh(pre_value):
    return jax.nn.gelu(pre_value, approximate=True)


def local(
    hidden_in,
    earlier,
    gain_attn,
    gain_mlp,
    w_qkv,
    w_out,
    w_up,
    w_down,
    mix_weights,
    lengths,
    slot_perm,
    grad_out,
):
    tensor_place = lax.axis_index("tensor")
    own_rows, width = hidden_in.shape
    slot_count = lengths.shape[0]
    group_rows = slot_perm.shape[0]
    slot_len = group_rows // slot_count
    shard_d = w_qkv.shape[0]
    head_cols = w_qkv.shape[2]

    hidden = hidden_in.astype(f32)
    normed_attn = layer_norm(hidden, gain_attn).astype(bf16)
    attn_pieces = gather_tensor(normed_attn)
    full_qkv = gather_dp(w_qkv.reshape(shard_d, 3 * head_cols))
    out_pieces = gather_tensor(w_out.T)
    full_out = gather_dp(jnp.concatenate(out_pieces, axis=1))
    full_up = gather_dp(w_up)
    full_down_t = gather_dp(w_down.T)

    first, position = slot_layout(lengths, slot_len)
    first = first.reshape(slot_count, 1, slot_len)
    cosine, sine = angle_tables(position.reshape(-1))
    perm = ((slot_perm // own_rows) ^ tensor_place) * own_rows + slot_perm % own_rows
    perm_col = perm[:, None]
    perm_row = perm[None, :]

    normed_slot, qkv = project(attn_pieces, perm_col, full_qkv, cosine, sine)
    *attended, stat = attend(qkv, first, perm_row, own_rows)
    heads_here = jnp.concatenate(exchange_tensor(attended), axis=1)
    after_attn = hidden + dot(heads_here, full_out, ((1,), (1,)))
    normed_mlp = layer_norm(after_attn, gain_mlp).astype(bf16)
    mlp_rows = jnp.concatenate(gather_tensor(normed_mlp), axis=0)

    cotangent = grad_out.astype(f32)
    own_grad = mix_weights[4] * cotangent
    grad_rows = jnp.concatenate(gather_tensor(own_grad.astype(bf16)), axis=0)

    pre_act = dot(mlp_rows, full_up)
    activated = gelu_tanh(pre_act).astype(bf16)
    grad_act = dot(grad_rows, full_down_t)
    unused_value, gelu_back = jax.vjp(gelu_tanh, pre_act)
    grad_pre = gelu_back(grad_act)[0].astype(bf16)
    partial = dot(grad_pre, full_up, ((1,), (1,)))
    grad_normed_mlp = scatter_tensor(
        [partial[k * own_rows : (k + 1) * own_rows] for k in range(4)]
    )
    partial_out = dot(activated, full_down_t, ((1,), (1,)))
    block_out = after_attn + scatter_tensor(
        [partial_out[k * own_rows : (k + 1) * own_rows] for k in range(4)]
    )
    grad_down_t = scatter_dp(dot(grad_rows, activated, ((0,), (0,))))
    grad_up = scatter_dp(dot(mlp_rows, grad_pre, ((0,), (0,))))

    unused_norm, second_back = jax.vjp(layer_norm, after_attn, gain_mlp)
    grad_resid_mlp, grad_gain_mlp = second_back(grad_normed_mlp)
    grad_after = own_grad + grad_resid_mlp
    grad_low = grad_after.astype(bf16)
    grad_heads = dot(grad_low, full_out).astype(bf16)
    grad_attended = exchange_tensor(
        [grad_heads[:, k * head_cols : (k + 1) * head_cols] for k in range(4)]
    )
    out_partial = dot(grad_low, heads_here, ((0,), (0,)))
    out_scattered = scatter_tensor(
        [out_partial[:, k * head_cols : (k + 1) * head_cols] for k in range(4)]
    )
    grad_out_t = scatter_dp(out_scattered)

    dqkv = attend_back(qkv, first, perm_col, grad_attended, stat, cosine, sine)
    attn_partial = unproject(dqkv, perm_row, full_qkv, own_rows)
    grad_normed_attn = scatter_tensor(
        [attn_partial[k * own_rows : (k + 1) * own_rows] for k in range(4)]
    )
    qkv_partial = dot(normed_slot, dqkv, ((0,), (0,)))
    grad_qkv = scatter_dp(qkv_partial)
    grad_gain_attn = jnp.sum(qkv_partial * full_qkv.astype(f32), axis=1) / gain_attn

    unused_first, first_back = jax.vjp(lambda value: layer_norm(value, gain_attn), hidden)
    grad_hidden = (grad_after + first_back(grad_normed_attn)[0]).astype(bf16)

    prior = [earlier[index].astype(f32) for index in range(4)]
    mixed_total = mix_weights[4] * block_out
    for index in range(4):
        mixed_total = mixed_total + mix_weights[index] * prior[index]
    grad_earlier = (mix_weights[:4, None, None] * cotangent[None]).astype(bf16)
    mix_terms = [jnp.sum(cotangent * value) for value in prior + [block_out]]
    spare = -(2 * width + 5) % 1024
    packed = jnp.concatenate(
        [grad_gain_attn, grad_gain_mlp, jnp.stack(mix_terms), jnp.zeros((spare,), f32)]
    )
    packed = total_all(packed.reshape(-1, LANES)).reshape(-1)
    return (
        mixed_total.astype(bf16),
        grad_hidden,
        grad_earlier,
        packed[:width],
        packed[width : 2 * width],
        grad_qkv.reshape(shard_d, 3, head_cols),
        grad_out_t.T,
        grad_up,
        grad_down_t.T,
        packed[2 * width : 2 * width + 5],
    )


def solution(mesh):
    rows = P(("dp", "tensor"), None)
    layers = P(None, ("dp", "tensor"), None)
    return jax.shard_map(
        local,
        mesh=mesh,
        in_specs=(
            rows,
            layers,
            P(),
            P(),
            P("dp", None, "tensor"),
            P("tensor", "dp"),
            P("dp", "tensor"),
            P("tensor", "dp"),
            P(),
            P("dp", None),
            P("dp"),
            rows,
        ),
        out_specs=(
            rows,
            rows,
            layers,
            P(),
            P(),
            P("dp", None, "tensor"),
            P("tensor", "dp"),
            P("dp", "tensor"),
            P("tensor", "dp"),
            P(),
        ),
        check_vma=False,
    )
```

time: 941 us -> 516 us (0.55)
  local copies, waits for them, and re-layouts: 201 us -> 25.7 us
  waiting for transfers between devices: 379 us -> 243 us
  matrix products: 129 us -> 47.9 us
  blocking collectives: 112 us -> 37.3 us
  Pallas kernels: 0 us -> 71.7 us
  other arithmetic: 87.5 us -> 45.1 us
  starting transfers between devices: 0.76 us -> 24.3 us
    reduce_scatter x7 -> x2, waiting for transfers between devices: 293 us -> 0.01 us  [scatter_dp(): lax.psum_scatter(value.astype(bf16), 'dp', scatter_dimension=0, tiled=True)]
    ppermute x0 -> x35, waiting for transfers between devices: none -> 125 us  [hop(): return lax.ppermute(value, axis, [(i, i ^ bit) for i in range(count)])]
    unnamed x15 -> x9, waiting for transfers between devices: 2.59 us -> 106 us
    gather x7 -> x0, local copies, waits for them, and re-layouts: 88.6 us -> none  [the longest x1 18.7 us: local(): jnp.take(grad_qkv, picked, axis=0)]
    dot_general x24 -> x10, matrix products: 122 us -> 47.9 us  [dot(): return lax.dot_general(a, b, (dims, ((), ())), preferred_element_type=f32)]
    pallas_call x0 -> x4, Pallas kernels: none -> 71.7 us  [the longest x1 22.4 us: attend_back(): pl.pallas_call(attend_back_kernel, grid=(slots,), in_specs=[pl.BlockSpec(...]
    all_gather x6 -> x3, waiting for transfers between devices: 82.4 us -> 11.4 us  [gather_dp(): return lax.all_gather(value, 'dp', axis=0, tiled=True)]
    dynamic_update_slice x8 -> x0, local copies, waits for them, and re-layouts: 60.5 us -> none  [local(): lax.map(lambda packed: attend_back(*packed), (by_slot(query), by_slot(key...]
  transfers between devices with their start and end apart: 14 -> 42, of which waited for: 9 -> 21; matrix products, arithmetic and copies ran while one was open for 34% -> 19% of each run, Pallas kernels for 0% -> 14%
where the time goes in v1:
time: 516 us; the launch traced here: 510 us
  waiting for transfers between devices  243 us (47%)
  Pallas kernels  71.7 us (14%)
  matrix products  47.9 us (9%)
  other arithmetic  45.1 us (9%)
  blocking collectives  37.3 us (7%)
  local copies, waits for them, and re-layouts  25.7 us (5%)
  starting transfers between devices  24.3 us (5%)
  between operations  15.1 us (3%)
    ppermute x35, waiting for transfers between devices, hop(): return lax.ppermute(value, axis, [(i, i ^ bit) for i in range(count)])  125 us
    unnamed x9, waiting for transfers between devices  106 us
    dot_general x10, matrix products, dot(): return lax.dot_general(a, b, (dims, ((), ())), preferred_element_type=f32)  47.9 us
    all_gather x1, blocking collectives, gather_dp(): return lax.all_gather(value, 'dp', axis=0, tiled=True)  37.3 us
    ppermute x35, starting transfers between devices, hop(): return lax.ppermute(value, axis, [(i, i ^ bit) for i in range(count)])  23.5 us
    pallas_call x1, Pallas kernels, attend_back(): pl.pallas_call(attend_back_kernel, grid=(slots,), in_specs=[pl.BlockSpec(...  22.4 us
    pallas_call x1, Pallas kernels, attend(): pl.pallas_call(attend_kernel, grid=(slots,), in_specs=[pl.BlockSpec((leng...  17.6 us
    pallas_call x1, Pallas kernels, project(): pl.pallas_call(project_kernel, grid=(rows // ROW_STEP,), in_specs=[whole]...  17.1 us
  transfers between devices with their start and end apart: 42, of which 21 were waited for; matrix products, arithmetic and copies ran while one was open for 19% of the time, Pallas kernels for 14%

profile of v1, /device:TPU:0, one launch (start us, length us, event | category | flops | bytes accessed | tf_op | source)
XLA Modules:
  0.0 509.8 jit_solution(12569971548590673610)
XLA Ops:
  8.2 3.0 collective-permute-start.7
  19.9 3.7 fusion.38
  23.7 13.7 %collective-permute-done.1.n2 = bf16[512,768]{1,0:T(8,128)(2,1)S(1)} collective-permute-done((bf16[512,768]{1,0:T(8,128)(2,1)S(1)}, bf16[512,768]{1,0:T(8,128)(2,1)S(1)}, u32[]{:S(2)}, u32[]{:S(2)}) %collective-permute-start.1) | collective-permute-done | bytes 786464 | tf_op jit(solution)/shard_map/ppermute | solution.py:272
  37.4 3.0 pad_maximum_fusion.2
  42.8 37.3 %all_gather.12.w_ref = bf16[768,576]{1,0:T(8,128)(2,1)} all-gather(bf16[96,576]{1,0:T(8,128)(2,1)S(1)} %copy.58), channel_id=1, replica_groups=mesh['dp'=8,'tensor'=4] {'dp'}, dimensions={0}, use_global_device_ids=true | all-gather | bytes 995328 | tf_op jit(solution)/shard_map/all_gather | solution.py:304
  81.0 17.1 %project.1 = (bf16[2048,768]{1,0:T(8,128)(2,1)}, bf16[2048,576]{1,0:T(8,128)(2,1)}) custom-call(bf16[512,768]{1,0:T(8,128)(2,1)} %copy-done.8, bf16[512,768]{1,0:T(8,128)(2,1)} %copy-done.13, bf16[512,768]{1,0:T(8,128)(2,1)} %copy-done.12, bf16[512,768]{1,0:T(8,128)(2,1)} %collective-permute-done.2.n3, s32[2048,1]{1,0:T(8,128)} %copy.60.perm_ref, ...), custom_call_target="tpu_custom_call" | custom-call | tf_op jit(solution)/shard_map/project/pallas_call | solution.py:89
  98.1 17.6 %attend.1 = (bf16[512,192]{1,0:T(8,128)(2,1)}, bf16[512,192]{1,0:T(8,128)(2,1)}, bf16[512,192]{1,0:T(8,128)(2,1)}, bf16[512,192]{1,0:T(8,128)(2,1)}, f32[2,8,1024]{2,1,0:T(8,128)}) custom-call(bf16[2048,576]{1,0:T(8,128)(2,1)} %get-tuple-element.17.qkv_ref, s32[2,1,1024]{2,1,0:T(1,128)} %reshape.128.first_ref, s32[1,2048]{1,0:T(1,128)} %bitcast.73), custom_call_target="tpu_custom_call" | custom-call | tf_op jit(solution)/shard_map/attend/pallas_call | solution.py:159
  117.6 7.6 %collective-permute-done.4 = bf16[512,192]{1,0:T(8,128)(2,1)S(1)} collective-permute-done((bf16[512,192]{1,0:T(8,128)(2,1)}, bf16[512,192]{1,0:T(8,128)(2,1)S(1)}, u32[]{:S(2)}, u32[]{:S(2)}) %collective-permute-start.4) | collective-permute-done | bytes 196640 | tf_op jit(solution)/shard_map/ppermute | solution.py:272
  125.2 4.5 collective-permute-done.5
  135.5 17.7 %collective-permute-done.10 = bf16[512,768]{1,0:T(8,128)(2,1)} collective-permute-done((bf16[512,768]{1,0:T(8,128)(2,1)S(1)}, bf16[512,768]{1,0:T(8,128)(2,1)}, u32[]{:S(2)}, u32[]{:S(2)}) %collective-permute-start.10) | collective-permute-done | bytes 786464 | tf_op jit(solution)/shard_map/ppermute | solution.py:272
  155.7 7.3 %fusion.37 = f32[2048,768]{1,0:T(8,128)} fusion(bf16[768,768]{1,0:T(8,128)(2,1)} %all-gather.6.cloned.1.call-done, bf16[512,768]{1,0:T(8,128)(2,1)} %collective-permute-done.11, bf16[512,768]{1,0:T(8,128)(2,1)} %collective-permute-done.10, bf16[512,768]{1,0:T(8,128)(2,1)} %collective-permute-done.9, bf16[512,768]{1,0:T(8,128)(2,1)S(1)} %multiply_convert_fusion.2), kind=kOutput, calls=%fused_computation.80 | convolution fusion | flops 2428502016 | bytes 10616832 | tf_op jit(solution)/shard_map/dot_general | solution.py:57
  163.0 11.4 %all-gather.8.cloned.1.call-done = bf16[768,768]{1,0:T(8,128)(2,1)} async-done(((bf16[96,768]{1,0:T(8,128)(2,1)}), bf16[768,768]{1,0:T(8,128)(2,1)}) %all-gather.8.cloned.1.call-update) | async-done | bytes 1179664 | tf_op jit(solution)/shard_map/all_gather | solution.py:304
  174.4 6.2 %fusion.65 = (bf16[2048,768]{1,0:T(8,128)(2,1)S(1)}, f32[2048,768]{1,0:T(8,128)S(1)}) fusion(bf16[768,768]{1,0:T(8,128)(2,1)} %all-gather.8.cloned.1.call-done, f32[2048,768]{1,0:T(8,128)} %fusion.37), kind=kOutput, calls=%fused_computation.133 | convolution fusion | flops 2431647744 | bytes 16908288 | tf_op jit(solution)/shard_map/dot_general | solution.py:57
  185.6 17.5 %collective-permute-done.14 = bf16[512,768]{1,0:T(8,128)(2,1)S(1)} collective-permute-done((bf16[512,768]{1,0:T(8,128)(2,1)S(1)}, bf16[512,768]{1,0:T(8,128)(2,1)S(1)}, u32[]{:S(2)}, u32[]{:S(2)}) %collective-permute-start.14) | collective-permute-done | bytes 786464 | tf_op jit(solution)/shard_map/ppermute | solution.py:272
  203.1 6.4 %fusion.21 = (f32[]{:T(128)}, f32[]{:T(128)}, f32[]{:T(128)}, f32[]{:T(128)}, bf16[512,768]{1,0:T(8,128)(2,1)}, /*index=5*/bf16[512,768]{1,0:T(8,128)(2,1)S(1)}) fusion(bf16[512,768]{1,0:T(8,128)(2,1)S(1)} %copy-done.1, bf16[4,512,768]{2,1,0:T(8,128)(2,1)S(1)} %copy-done.9, f32[]{:T(128)} %bitcast.12, f32[]{:T(128)} %bitcast.10, f32[]{:T(128)} %bitcast.8, ...), kind=kLoop, calls=%fused_computation.43 | loop fusion | flops 11796476 | bytes 10223652 | tf_op jit(solution)/shard_map/reduce_sum | solution.py:411
  211.0 17.3 %collective-permute-done.16 = bf16[512,768]{1,0:T(8,128)(2,1)S(1)} collective-permute-done((bf16[512,768]{1,0:T(8,128)(2,1)S(1)}, bf16[512,768]{1,0:T(8,128)(2,1)S(1)}, u32[]{:S(2)}, u32[]{:S(2)}) %collective-permute-start.16) | collective-permute-done | bytes 786464 | tf_op jit(solution)/shard_map/ppermute | solution.py:272
  231.4 4.0 convolution_convert_fusion
  235.7 10.1 %fusion.6 = bf16[2048,768]{1,0:T(8,128)(2,1)S(1)} fusion(f32[2048,768]{1,0:T(8,128)} %fusion.37, bf16[768,768]{1,0:T(8,128)(2,1)} %all-gather.8.cloned.1.call-done, bf16[512,768]{1,0:T(8,128)(2,1)} %copy-done.36, bf16[512,768]{1,0:T(8,128)(2,1)} %copy-done.34, bf16[512,768]{1,0:T(8,128)(2,1)} %copy-done.35, bf16[512,768]{1,0:T(8,128)(2,1)} %copy-done.14), kind=kOutput, calls=%fused_computation.8 | convolution fusion | flops 2459959296 | bytes 13762560 | tf_op jit(solution)/shard_map/dot_general | solution.py:57
  254.5 5.3 %convolution_convert_fusion.1 = bf16[768,768]{1,0:T(8,128)(2,1)} fusion(bf16[2048,768]{1,0:T(8,128)(2,1)S(1)} %fusion.6, bf16[512,768]{1,0:T(8,128)(2,1)} %collective-permute-done.11, bf16[512,768]{1,0:T(8,128)(2,1)} %collective-permute-done.10, bf16[512,768]{1,0:T(8,128)(2,1)} %collective-permute-done.9, bf16[512,768]{1,0:T(8,128)(2,1)S(1)} %copy-done.16), kind=kOutput, calls=%fused_computation.66 | convolution fusion | flops 2429091840 | bytes 7471104 | tf_op jit(solution)/shard_map/dot_general | solution.py:57
  259.9 13.0 %collective-permute-done.20 = bf16[512,768]{1,0:T(8,128)(2,1)} collective-permute-done((bf16[512,768]{1,0:T(8,128)(2,1)}, bf16[512,768]{1,0:T(8,128)(2,1)}, u32[]{:S(2)}, u32[]{:S(2)}) %collective-permute-start.20) | collective-permute-done | bytes 786464 | tf_op jit(solution)/shard_map/ppermute | solution.py:272
  272.9 4.6 multiply_reduce_fusion.1
  288.9 4.0 collective-permute-done.22.d2
  292.9 4.7 collective-permute-done.23.d3
  298.3 22.4 %attend_back.1.dqkv_ref = bf16[2048,576]{1,0:T(8,128)(2,1)} custom-call(bf16[2048,576]{1,0:T(8,128)(2,1)} %get-tuple-element.17.qkv_ref, s32[2,1,1024]{2,1,0:T(1,128)} %reshape.128.first_ref, s32[2048,1]{1,0:T(8,128)} %copy.60.perm_ref, bf16[512,192]{1,0:T(8,128)(2,1)} %get-tuple-element.98.d0, bf16[512,192]{1,0:T(8,128)(2,1)} %copy-done.17, ...), custom_call_target="tpu_custom_call" | custom-call | tf_op jit(solution)/shard_map/attend_back/pallas_call | solution.py:226
  320.7 6.3 %fusion.67 = (bf16[768,576]{0,1:T(8,128)(2,1)}, f32[768,576]{0,1:T(8,128)}) fusion(bf16[2048,768]{1,0:T(8,128)(2,1)} %get-tuple-element.23, bf16[2048,576]{1,0:T(8,128)(2,1)} %attend_back.1.dqkv_ref), kind=kOutput, calls=%fused_computation.135 | convolution fusion | flops 1812381696 | bytes 8159232 | tf_op jit(solution)/shard_map/dot_general | solution.py:57
  327.0 2.9 copy.66
  331.7 14.5 %unproject.1 = bf16[2048,768]{1,0:T(8,128)(2,1)} custom-call(bf16[2048,576]{1,0:T(8,128)(2,1)} %attend_back.1.dqkv_ref, s32[1,2048]{1,0:T(1,128)} %bitcast.74, bf16[768,576]{1,0:T(8,128)(2,1)} %all_gather.12.w_ref), custom_call_target="tpu_custom_call" | custom-call | tf_op jit(solution)/shard_map/unproject/pallas_call | solution.py:256
  346.3 3.3 concatenate.27
  355.1 7.5 %collective-permute-done.28 = f32[16,128]{1,0:T(8,128)S(1)} collective-permute-done((f32[16,128]{1,0:T(8,128)S(1)}, f32[16,128]{1,0:T(8,128)S(1)}, u32[]{:S(2)}, u32[]{:S(2)}) %collective-permute-start.28) | collective-permute-done | bytes 8224 | tf_op jit(solution)/shard_map/ppermute | solution.py:272
  363.2 3.1 collective-permute-done.29
  386.1 48.1 %reduce-scatter.15.cloned.1.call-done = bf16[96,192]{1,0:T(8,128)(2,1)} async-done(((bf16[768,192]{1,0:T(8,128)(2,1)}), bf16[96,192]{1,0:T(8,128)(2,1)}) %reduce-scatter.15.cloned.1.call-update) | async-done | bytes 36880
  442.5 58.1 %reduce-scatter.13.cloned.1.call-done = bf16[96,576]{1,0:T(8,128)(2,1)} async-done(((bf16[768,576]{1,0:T(8,128)(2,1)}), bf16[96,576]{1,0:T(8,128)(2,1)}) %reduce-scatter.13.cloned.1.call-update) | async-done | bytes 110608
  (220 shorter events, 91.3 us)
Async XLA Ops:
  7.2 122.6 %all-gather.4.cloned.1.call-start = ((), (), s32[]{:S(2)}) async-start(), calls=%async_computation.4 | async-start | bytes 1327104 | tf_op jit(solution)/shard_map/all_gather | solution.py:304
  8.2 5.1 %collective-permute-start.7 = (bf16[96,192]{1,0:T(8,128)(2,1)S(1)}, bf16[96,192]{1,0:T(8,128)(2,1)S(1)}, u32[]{:S(2)}, u32[]{:S(2)}) collective-permute-start(bf16[96,192]{1,0:T(8,128)(2,1)S(1)} %bitcast.68), channel_id=1, source_target_pairs={{0,2},{1,3},{2,0},{3,1},{4,6},{5,7},{6,4},{7,5},{8,10},{9,11},{10,... | collective-permute-start | bytes 110600 | tf_op jit(solution)/shard_map/ppermute | solution.py:272
  15.3 137.8 %all-gather.6.cloned.1.call-start = ((), (), s32[]{:S(2)}) async-start(), calls=%async_computation.5 | async-start | bytes 1327104 | tf_op jit(solution)/shard_map/all_gather | solution.py:304
  17.4 20.0 %collective-permute-start.1 = (bf16[512,768]{1,0:T(8,128)(2,1)S(1)}, bf16[512,768]{1,0:T(8,128)(2,1)S(1)}, u32[]{:S(2)}, u32[]{:S(2)}) collective-permute-start(bf16[512,768]{1,0:T(8,128)(2,1)S(1)} %fusion.25.n0), channel_id=1, source_target_pairs={{0,2},{1,3},{2,0},{3,1},{4,6},{5,7},{6,4},{7,5},{8,10},{9,11},{10,... | collective-permute-start | bytes 2359304 | tf_op jit(solution)/shard_map/ppermute | solution.py:272
  19.5 60.6 %collective-permute-start = (bf16[512,768]{1,0:T(8,128)(2,1)S(1)}, bf16[512,768]{1,0:T(8,128)(2,1)S(1)}, u32[]{:S(2)}, u32[]{:S(2)}) collective-permute-start(bf16[512,768]{1,0:T(8,128)(2,1)S(1)} %fusion.25.n0), channel_id=1, source_target_pairs={{0,1},{1,0},{2,3},{3,2},{4,5},{5,4},{6,7},{7,6},{8,9},{9,8},{10,11... | collective-permute-start | bytes 2359304 | tf_op jit(solution)/shard_map/ppermute | solution.py:272
  19.5 154.9 %all-gather.8.cloned.1.call-start = ((), (), s32[]{:S(2)}) async-start(), calls=%async_computation.6 | async-start | bytes 1327104 | tf_op jit(solution)/shard_map/all_gather | solution.py:304
  37.4 42.7 %collective-permute-start.2 = (bf16[512,768]{1,0:T(8,128)(2,1)S(1)}, bf16[512,768]{1,0:T(8,128)(2,1)}, u32[]{:S(2)}, u32[]{:S(2)}) collective-permute-start(bf16[512,768]{1,0:T(8,128)(2,1)S(1)} %collective-permute-done.1.n2), channel_id=1, source_target_pairs={{0,1},{1,0},{2,3},{3,2},{4,5},{5,4},{6,7},{7,6},{8,9},{9,8},{10,11... | collective-permute-start | bytes 2359304 | tf_op jit(solution)/shard_map/ppermute | solution.py:272
  115.8 9.5 %collective-permute-start.4 = (bf16[512,192]{1,0:T(8,128)(2,1)}, bf16[512,192]{1,0:T(8,128)(2,1)S(1)}, u32[]{:S(2)}, u32[]{:S(2)}) collective-permute-start(bf16[512,192]{1,0:T(8,128)(2,1)} %get-tuple-element.20), channel_id=1, source_target_pairs={{0,2},{1,3},{2,0},{3,1},{4,6},{5,7},{6,4},{7,5},{8,10},{9,11},{10,... | collective-permute-start | bytes 589832 | tf_op jit(solution)/shard_map/ppermute | solution.py:272
  117.5 12.3 %collective-permute-start.5 = (bf16[512,192]{1,0:T(8,128)(2,1)}, bf16[512,192]{1,0:T(8,128)(2,1)S(1)}, u32[]{:S(2)}, u32[]{:S(2)}) collective-permute-start(bf16[512,192]{1,0:T(8,128)(2,1)} %get-tuple-element.21), channel_id=1, source_target_pairs={{0,3},{1,2},{2,1},{3,0},{4,7},{5,6},{6,5},{7,4},{8,11},{9,10},{10,... | collective-permute-start | bytes 589832 | tf_op jit(solution)/shard_map/ppermute | solution.py:272
  133.1 20.0 %collective-permute-start.10 = (bf16[512,768]{1,0:T(8,128)(2,1)S(1)}, bf16[512,768]{1,0:T(8,128)(2,1)}, u32[]{:S(2)}, u32[]{:S(2)}) collective-permute-start(bf16[512,768]{1,0:T(8,128)(2,1)S(1)} %multiply_convert_fusion.2), channel_id=1, source_target_pairs={{0,2},{1,3},{2,0},{3,1},{4,6},{5,7},{6,4},{7,5},{8,10},{9,11},{10,... | collective-permute-start | bytes 2359304 | tf_op jit(solution)/shard_map/ppermute | solution.py:272
  134.9 247.9 %reduce-scatter.11.cloned.1.call-start = ((), (), s32[]{:S(2)}) async-start(), calls=%async_computation.8 | async-start | bytes 1327104 | tf_op jit(solution)/shard_map/reduce_scatter | solution.py:308
  135.3 17.8 %collective-permute-start.9 = (bf16[512,768]{1,0:T(8,128)(2,1)S(1)}, bf16[512,768]{1,0:T(8,128)(2,1)}, u32[]{:S(2)}, u32[]{:S(2)}) collective-permute-start(bf16[512,768]{1,0:T(8,128)(2,1)S(1)} %multiply_convert_fusion.2), channel_id=1, source_target_pairs={{0,1},{1,0},{2,3},{3,2},{4,5},{5,4},{6,7},{7,6},{8,9},{9,8},{10,11... | collective-permute-start | bytes 2359304 | tf_op jit(solution)/shard_map/ppermute | solution.py:272
  183.4 19.6 %collective-permute-start.14 = (bf16[512,768]{1,0:T(8,128)(2,1)S(1)}, bf16[512,768]{1,0:T(8,128)(2,1)S(1)}, u32[]{:S(2)}, u32[]{:S(2)}) collective-permute-start(bf16[512,768]{1,0:T(8,128)(2,1)S(1)} %fusion.29), channel_id=1, source_target_pairs={{0,2},{1,3},{2,0},{3,1},{4,6},{5,7},{6,4},{7,5},{8,10},{9,11},{10,... | collective-permute-start | bytes 2359304 | tf_op jit(solution)/shard_map/ppermute | solution.py:272
  209.5 18.7 %collective-permute-start.16 = (bf16[512,768]{1,0:T(8,128)(2,1)S(1)}, bf16[512,768]{1,0:T(8,128)(2,1)S(1)}, u32[]{:S(2)}, u32[]{:S(2)}) collective-permute-start(bf16[512,768]{1,0:T(8,128)(2,1)S(1)} %get-tuple-element.94), channel_id=1, source_target_pairs={{0,2},{1,3},{2,0},{3,1},{4,6},{5,7},{6,4},{7,5},{8,10},{9,11},{10,... | collective-permute-start | bytes 2359304 | tf_op jit(solution)/shard_map/ppermute | solution.py:272
  211.0 17.3 %collective-permute-start.15 = (bf16[512,768]{1,0:T(8,128)(2,1)S(1)}, bf16[512,768]{1,0:T(8,128)(2,1)S(1)}, u32[]{:S(2)}, u32[]{:S(2)}) collective-permute-start(bf16[512,768]{1,0:T(8,128)(2,1)S(1)} %get-tuple-element.94), channel_id=1, source_target_pairs={{0,1},{1,0},{2,3},{3,2},{4,5},{5,4},{6,7},{7,6},{8,9},{9,8},{10,11... | collective-permute-start | bytes 2359304 | tf_op jit(solution)/shard_map/ppermute | solution.py:272
  235.5 148.9 %reduce-scatter.9.cloned.1.call-start = ((), (), s32[]{:S(2)}) async-start(), calls=%async_computation.7 | async-start | bytes 1327104 | tf_op jit(solution)/shard_map/reduce_scatter | solution.py:308
  249.7 10.1 %collective-permute-start.18 = (bf16[512,768]{1,0:T(8,128)(2,1)}, bf16[512,768]{1,0:T(8,128)(2,1)}, u32[]{:S(2)}, u32[]{:S(2)}) collective-permute-start(bf16[512,768]{1,0:T(8,128)(2,1)} %get-tuple-element.88), channel_id=1, source_target_pairs={{0,1},{1,0},{2,3},{3,2},{4,5},{5,4},{6,7},{7,6},{8,9},{9,8},{10,11... | collective-permute-start | bytes 2359304 | tf_op jit(solution)/shard_map/ppermute | solution.py:272
  253.0 19.9 %collective-permute-start.20 = (bf16[512,768]{1,0:T(8,128)(2,1)}, bf16[512,768]{1,0:T(8,128)(2,1)}, u32[]{:S(2)}, u32[]{:S(2)}) collective-permute-start(bf16[512,768]{1,0:T(8,128)(2,1)} %fusion.27), channel_id=1, source_target_pairs={{0,2},{1,3},{2,0},{3,1},{4,6},{5,7},{6,4},{7,5},{8,10},{9,11},{10,... | collective-permute-start | bytes 2359304 | tf_op jit(solution)/shard_map/ppermute | solution.py:272
  259.8 174.4 %reduce-scatter.15.cloned.1.call-start = ((), (), s32[]{:S(2)}) async-start(), calls=%async_computation.10 | async-start | bytes 442368
  283.7 5.2 %collective-permute-start.21 = (bf16[512,192]{1,0:T(8,128)(2,1)S(1)}, bf16[512,192]{1,0:T(8,128)(2,1)S(1)}, u32[]{:S(2)}, u32[]{:S(2)}) collective-permute-start(bf16[512,192]{1,0:T(8,128)(2,1)S(1)} %get-tuple-element.97), channel_id=1, source_target_pairs={{0,1},{1,0},{2,3},{3,2},{4,5},{5,4},{6,7},{7,6},{8,9},{9,8},{10,11... | collective-permute-start | bytes 589832 | tf_op jit(solution)/shard_map/ppermute | solution.py:272
  283.7 9.2 %collective-permute-start.22 = (bf16[512,192]{1,0:T(8,128)(2,1)S(1)}, bf16[512,192]{1,0:T(8,128)(2,1)S(1)}, u32[]{:S(2)}, u32[]{:S(2)}) collective-permute-start(bf16[512,192]{1,0:T(8,128)(2,1)S(1)} %get-tuple-element.96), channel_id=1, source_target_pairs={{0,2},{1,3},{2,0},{3,1},{4,6},{5,7},{6,4},{7,5},{8,10},{9,11},{10,... | collective-permute-start | bytes 589832 | tf_op jit(solution)/shard_map/ppermute | solution.py:272
  285.2 12.4 %collective-permute-start.23 = (bf16[512,192]{1,0:T(8,128)(2,1)S(1)}, bf16[512,192]{1,0:T(8,128)(2,1)S(1)}, u32[]{:S(2)}, u32[]{:S(2)}) collective-permute-start(bf16[512,192]{1,0:T(8,128)(2,1)S(1)} %get-tuple-element.95), channel_id=1, source_target_pairs={{0,3},{1,2},{2,1},{3,0},{4,7},{5,6},{6,5},{7,4},{8,11},{9,10},{10,... | collective-permute-start | bytes 589832 | tf_op jit(solution)/shard_map/ppermute | solution.py:272
  288.4 64.6 %collective-permute-start.33 = (bf16[768,192]{0,1:T(8,128)(2,1)S(1)}, bf16[768,192]{0,1:T(8,128)(2,1)S(1)}, u32[]{:S(2)}, u32[]{:S(2)}) collective-permute-start(bf16[768,192]{0,1:T(8,128)(2,1)S(1)} %get-tuple-element.93), channel_id=1, source_target_pairs={{0,1},{1,0},{2,3},{3,2},{4,5},{5,4},{6,7},{7,6},{8,9},{9,8},{10,11... | collective-permute-start | bytes 884744 | tf_op jit(solution)/shard_map/ppermute | solution.py:272
  288.7 82.2 %collective-permute-start.32 = (bf16[768,192]{0,1:T(8,128)(2,1)S(1)}, bf16[768,192]{0,1:T(8,128)(2,1)}, u32[]{:S(2)}, u32[]{:S(2)}) collective-permute-start(bf16[768,192]{0,1:T(8,128)(2,1)S(1)} %get-tuple-element.92), channel_id=1, source_target_pairs={{0,1},{1,0},{2,3},{3,2},{4,5},{5,4},{6,7},{7,6},{8,9},{9,8},{10,11... | collective-permute-start | bytes 884744 | tf_op jit(solution)/shard_map/ppermute | solution.py:272
  349.5 5.0 collective-permute-start.27
  352.9 20.1 %collective-permute-start.25 = (bf16[512,768]{1,0:T(8,128)(2,1)}, bf16[512,768]{1,0:T(8,128)(2,1)}, u32[]{:S(2)}, u32[]{:S(2)}) collective-permute-start(bf16[512,768]{1,0:T(8,128)(2,1)} %get-tuple-element.87), channel_id=1, source_target_pairs={{0,1},{1,0},{2,3},{3,2},{4,5},{5,4},{6,7},{7,6},{8,9},{9,8},{10,11... | collective-permute-start | bytes 2359304 | tf_op jit(solution)/shard_map/ppermute | solution.py:272
  353.0 17.9 %collective-permute-start.34 = (bf16[768,192]{0,1:T(8,128)(2,1)S(1)}, bf16[768,192]{0,1:T(8,128)(2,1)S(1)}, u32[]{:S(2)}, u32[]{:S(2)}) collective-permute-start(bf16[768,192]{0,1:T(8,128)(2,1)S(1)} %fusion.33), channel_id=1, source_target_pairs={{0,2},{1,3},{2,0},{3,1},{4,6},{5,7},{6,4},{7,5},{8,10},{9,11},{10,... | collective-permute-start | bytes 884744 | tf_op jit(solution)/shard_map/ppermute | solution.py:272
  354.6 8.0 %collective-permute-start.28 = (f32[16,128]{1,0:T(8,128)S(1)}, f32[16,128]{1,0:T(8,128)S(1)}, u32[]{:S(2)}, u32[]{:S(2)}) collective-permute-start(f32[16,128]{1,0:T(8,128)S(1)} %bitcast_add_fusion), channel_id=1, source_target_pairs={{0,2},{1,3},{2,0},{3,1},{4,6},{5,7},{6,4},{7,5},{8,10},{9,11},{10,... | collective-permute-start | bytes 24584 | tf_op jit(solution)/shard_map/ppermute | solution.py:272
  367.2 68.6 %collective-permute-start.24 = (bf16[512,768]{1,0:T(8,128)(2,1)}, bf16[512,768]{1,0:T(8,128)(2,1)}, u32[]{:S(2)}, u32[]{:S(2)}) collective-permute-start(bf16[512,768]{1,0:T(8,128)(2,1)} %get-tuple-element.86), channel_id=1, source_target_pairs={{0,1},{1,0},{2,3},{3,2},{4,5},{5,4},{6,7},{7,6},{8,9},{9,8},{10,11... | collective-permute-start | bytes 2359304 | tf_op jit(solution)/shard_map/ppermute | solution.py:272
  369.9 11.7 %collective-permute-start.31 = (f32[16,128]{1,0:T(8,128)S(1)}, f32[16,128]{1,0:T(8,128)S(1)}, u32[]{:S(2)}, u32[]{:S(2)}) collective-permute-start(f32[16,128]{1,0:T(8,128)S(1)} %add.150), channel_id=1, source_target_pairs={{0,16},{4,20},{8,24},{12,28},{16,0},{20,4},{24,8},{28,12},{1,17},{... | collective-permute-start | bytes 24584 | tf_op jit(solution)/shard_map/ppermute | solution.py:272
  372.9 127.7 %reduce-scatter.13.cloned.1.call-start = ((), (), s32[]{:S(2)}) async-start(), calls=%async_computation.9 | async-start | bytes 1105920
  375.4 60.4 %collective-permute-start.26 = (bf16[512,768]{1,0:T(8,128)(2,1)}, bf16[512,768]{1,0:T(8,128)(2,1)}, u32[]{:S(2)}, u32[]{:S(2)}) collective-permute-start(bf16[512,768]{1,0:T(8,128)(2,1)} %add_convert_fusion.1), channel_id=1, source_target_pairs={{0,2},{1,3},{2,0},{3,1},{4,6},{5,7},{6,4},{7,5},{8,10},{9,11},{10,... | collective-permute-start | bytes 2359304 | tf_op jit(solution)/shard_map/ppermute | solution.py:272
  (49 other events, 415.1 us)
Sparse Core Ops, SparseCore 0:
  15.4 49.4 all-gather.3
  67.1 38.7 all-gather.5
  135.0 39.4 all-gather.7
  235.6 63.3 reduce-scatter.10
  302.3 63.7 reduce-scatter.8
  373.0 61.1 reduce-scatter.14
  437.6 63.0 reduce-scatter.12

commit v2 on v1

--- a/solution.py
+++ b/solution.py
@@ -4,6 +4,7 @@
 from jax.experimental import pallas as pl
 from jax.experimental.pallas import tpu as pltpu
 from jax.sharding import PartitionSpec as P
+
 
 HEAD_SIZE = 64
 HALF = HEAD_SIZE // 2
@@ -57,20 +58,37 @@
     return lax.dot_general(a, b, (dims, ((), ())), preferred_element_type=f32)
 
 
-def project_kernel(n0, n1, n2, n3, perm_ref, w_ref, cos_ref, sin_ref, slot_ref, qkv_ref):
-    pieces = (n0, n1, n2, n3)
-    rows = perm_ref.shape[0]
-    each = n0.shape[0]
-    wanted = perm_ref[...]
+def order_kernel(n0, n1, n2, n3, perm_ref, slot_ref):
+    slot_ref[...] = pick_rows(perm_ref[...], (n0, n1, n2, n3)).astype(bf16)
+
+
+def pick_rows(wanted, pieces):
+    each = pieces[0].shape[0]
     total = None
     for k in range(4):
-        here = lax.broadcasted_iota(jnp.int32, (rows, each), 1) + k * each
+        here = lax.broadcasted_iota(jnp.int32, (wanted.shape[0], each), 1) + k * each
         pick = jnp.where(here == wanted, 1.0, 0.0).astype(bf16)
         part = dot(pick, pieces[k][...])
         total = part if total is None else total + part
-    normed = total.astype(bf16)
-    slot_ref[...] = normed
-    qkv = dot(normed, w_ref[...])
+    return total
+
+
+def to_slots(pieces, perm_col):
+    each, width = pieces[0].shape
+    rows = perm_col.shape[0]
+    whole = pl.BlockSpec((each, width), lambda i: (0, 0))
+    return pl.pallas_call(
+        order_kernel,
+        grid=(rows // ROW_STEP,),
+        in_specs=[whole] * 4 + [pl.BlockSpec((ROW_STEP, 1), lambda i: (i, 0))],
+        out_specs=pl.BlockSpec((ROW_STEP, width), lambda i: (i, 0)),
+        out_shape=jax.ShapeDtypeStruct((rows, width), bf16),
+        name="to_slots",
+    )(*pieces, perm_col)
+
+
+def project_kernel(normed_ref, w_ref, cos_ref, sin_ref, qkv_ref):
+    qkv = dot(normed_ref[...], w_ref[...])
     cosine = cos_ref[...]
     sine = sin_ref[...]
     third = qkv.shape[1] // 3
@@ -81,31 +99,117 @@
     qkv_ref[:, 2 * third :] = qkv[:, 2 * third :].astype(bf16)
 
 
-def project(pieces, perm_col, w, cosine, sine):
-    each, width = pieces[0].shape
-    rows = perm_col.shape[0]
+def project(normed, w, cosine, sine):
+    rows, width = normed.shape
     cols = w.shape[1]
-    whole = pl.BlockSpec((each, width), lambda i: (0, 0))
+    step = 2 * ROW_STEP
     return pl.pallas_call(
         project_kernel,
-        grid=(rows // ROW_STEP,),
-        in_specs=[whole] * 4
+        grid=(rows // step,),
+        in_specs=[
+            pl.BlockSpec((step, width), lambda i: (i, 0)),
+            pl.BlockSpec(w.shape, lambda i: (0, 0)),
+            pl.BlockSpec((step, LANES), lambda i: (i, 0)),
+            pl.BlockSpec((step, LANES), lambda i: (i, 0)),
+        ],
+        out_specs=pl.BlockSpec((step, cols), lambda i: (i, 0)),
+        out_shape=jax.ShapeDtypeStruct((rows, cols), bf16),
+        name="project",
+    )(normed, w, cosine, sine)
+
+
+def mlp_kernel(a_ref, b_ref, ga_ref, gb_ref, up_ref, down_ref, *outs):
+    c = 0.7978845608028654
+    for n, (rows_ref, grad_ref) in enumerate(((a_ref, ga_ref), (b_ref, gb_ref))):
+        dn_ref, hid_ref, du_ref = outs[3 * n : 3 * n + 3]
+        u = dot(rows_ref[...], up_ref[...])
+        square = u * u
+        t = jnp.tanh(c * (u * (1.0 + 0.044715 * square)))
+        half = 0.5 * (1.0 + t)
+        hid_ref[...] = (u * half).astype(bf16)
+        slope = half + 0.5 * u * (1.0 - t * t) * (c * (1.0 + 3 * 0.044715 * square))
+        du = (dot(grad_ref[...], down_ref[...]) * slope).astype(bf16)
+        du_ref[...] = du
+        dn_ref[...] = dot(du, up_ref[...], ((1,), (1,))).astype(bf16)
+
+
+def mlp(rows, grads, updown):
+    each, width = rows[0].shape
+    units = updown.shape[1] // 2
+    block = pl.BlockSpec((ROW_STEP, width), lambda i: (i, 0))
+    inner = pl.BlockSpec((ROW_STEP, units), lambda i: (i, 0))
+    wide = jax.ShapeDtypeStruct((each, width), bf16)
+    mid = jax.ShapeDtypeStruct((each, units), bf16)
+    return pl.pallas_call(
+        mlp_kernel,
+        grid=(each // ROW_STEP,),
+        in_specs=[block] * 4
         + [
-            pl.BlockSpec((ROW_STEP, 1), lambda i: (i, 0)),
-            pl.BlockSpec(w.shape, lambda i: (0, 0)),
-            pl.BlockSpec((ROW_STEP, LANES), lambda i: (i, 0)),
-            pl.BlockSpec((ROW_STEP, LANES), lambda i: (i, 0)),
+            pl.BlockSpec((width, units), lambda i: (0, 0)),
+            pl.BlockSpec((width, units), lambda i: (0, 1)),
         ],
-        out_specs=[
-            pl.BlockSpec((ROW_STEP, width), lambda i: (i, 0)),
-            pl.BlockSpec((ROW_STEP, cols), lambda i: (i, 0)),
-        ],
-        out_shape=[
-            jax.ShapeDtypeStruct((rows, width), bf16),
-            jax.ShapeDtypeStruct((rows, cols), bf16),
-        ],
-        name="project",
-    )(*pieces, perm_col, w, cosine, sine)
+        out_specs=[block, inner, inner] * 2,
+        out_shape=[wide, mid, mid] * 2,
+    )(*rows, *grads, updown, updown)
+
+
+def mlp_out_kernel(h0, h1, h2, h3, down_ref, o0, o1, o2, o3):
+    for hid_ref, out_ref in ((h3, o3), (h2, o2), (h1, o1), (h0, o0)):
+        out_ref[...] = dot(hid_ref[...], down_ref[...], ((1,), (1,))).astype(bf16)
+
+
+def mlp_out(hids, updown):
+    each, units = hids[0].shape
+    width = updown.shape[0]
+    return pl.pallas_call(
+        mlp_out_kernel,
+        grid=(each // ROW_STEP,),
+        in_specs=[pl.BlockSpec((ROW_STEP, units), lambda i: (i, 0))] * 4
+        + [pl.BlockSpec((width, units), lambda i: (0, 1))],
+        out_specs=[pl.BlockSpec((ROW_STEP, width), lambda i: (i, 0))] * 4,
+        out_shape=[jax.ShapeDtypeStruct((each, width), bf16)] * 4,
+        name="mlp_out",
+    )(*hids, updown)
+
+
+def mlp_weights_kernel(*refs):
+    rows, grads, hids, dus = refs[:4], refs[4:8], refs[8:12], refs[12:16]
+    out_ref, acc = refs[16:]
+    units = hids[0].shape[1]
+    step = pl.program_id(0)
+
+    @pl.when(step == 0)
+    def _():
+        acc[...] = jnp.zeros(acc.shape, f32)
+
+    up = down = None
+    for k in range(4):
+        a = dot(rows[k][...], dus[k][...], ((0,), (0,)))
+        b = dot(grads[k][...], hids[k][...], ((0,), (0,)))
+        up = a if up is None else up + a
+        down = b if down is None else down + b
+    acc[:, :units] += up
+    acc[:, units:] += down
+
+    @pl.when(step == pl.num_programs(0) - 1)
+    def _():
+        out_ref[...] = acc[...].astype(bf16)
+
+
+def mlp_weights(rows, grads, hids, dus):
+    each, width = rows[0].shape
+    units = hids[0].shape[1]
+    block = pl.BlockSpec((ROW_STEP, width), lambda i: (i, 0))
+    inner = pl.BlockSpec((ROW_STEP, units), lambda i: (i, 0))
+    return pl.pallas_call(
+        mlp_weights_kernel,
+        grid=(each // ROW_STEP,),
+        in_specs=[block] * 8 + [inner] * 8,
+        out_specs=pl.BlockSpec((width, 2 * units), lambda i: (0, 0)),
+        out_shape=jax.ShapeDtypeStruct((width, 2 * units), bf16),
+        scratch_shapes=[pltpu.VMEM((width, 2 * units), f32)],
+        name="mlp_weights",
+    )(*rows, *grads, *hids, *dus)
 
 
 def spread_rows(perm_ref, value, start, count):
@@ -179,15 +283,9 @@
     third = cols // 3
     scale = HEAD_SIZE ** (-0.5)
     factor = scale * LOG2E
-    each = d0.shape[0]
     for start in range(0, length, ROW_STEP):
-        total = None
-        for k, ref in enumerate((d0, d1, d2, d3)):
-            here = lax.broadcasted_iota(jnp.int32, (ROW_STEP, each), 1) + k * each
-            pick = jnp.where(here == perm_ref[start : start + ROW_STEP, :], 1.0, 0.0).astype(bf16)
-            part = dot(pick, ref[...])
-            total = part if total is None else total + part
-        given[start : start + ROW_STEP, :] = total.astype(bf16)
+        wanted = perm_ref[start : start + ROW_STEP, :]
+        given[start : start + ROW_STEP, :] = pick_rows(wanted, (d0, d1, d2, d3)).astype(bf16)
     acc[:, third:] = jnp.zeros((length, 2 * third), f32)
     for head in range(third // HEAD_SIZE):
         at = head * HEAD_SIZE
@@ -244,26 +342,26 @@
     )(qkv, first, perm_col, *grads, stat, cosine, sine)
 
 
-def unproject(dqkv, perm_row, w, each):
+def unproject(dqkv, perm_row, w, each, first):
     rows, cols = dqkv.shape
     width = w.shape[0]
 
-    def kernel(dqkv_ref, perm_ref, w_ref, out_ref):
-        start = pl.program_id(0) * ROW_STEP
-        picked = spread_rows(perm_ref, dqkv_ref[...], start, ROW_STEP).astype(bf16)
-        out_ref[...] = dot(picked, w_ref[...], ((1,), (1,))).astype(bf16)
+    def kernel(dqkv_ref, perm_ref, w_ref, a_ref, b_ref):
+        for k, out_ref in ((first + 1, b_ref), (first, a_ref)):
+            start = k * each + pl.program_id(0) * ROW_STEP
+            picked = spread_rows(perm_ref, dqkv_ref[...], start, ROW_STEP).astype(bf16)
+            out_ref[...] = dot(picked, w_ref[...], ((1,), (1,))).astype(bf16)
 
     return pl.pallas_call(
         kernel,
-        grid=(rows // ROW_STEP,),
+        grid=(each // ROW_STEP,),
         in_specs=[
             pl.BlockSpec((rows, cols), lambda i: (0, 0)),
             pl.BlockSpec((1, rows), lambda i: (0, 0)),
             pl.BlockSpec(w.shape, lambda i: (0, 0)),
         ],
-        out_specs=pl.BlockSpec((ROW_STEP, width), lambda i: (i, 0)),
-        out_shape=jax.ShapeDtypeStruct((rows, width), bf16),
-        name="unproject",
+        out_specs=[pl.BlockSpec((ROW_STEP, width), lambda i: (i, 0))] * 2,
+        out_shape=[jax.ShapeDtypeStruct((each, width), bf16)] * 2,
     )(dqkv, perm_row, w)
 
 
@@ -273,21 +371,22 @@
 
 
 def gather_tensor(value):
+    near = hop(value, "tensor", 1)
     far = hop(value, "tensor", 2)
-    near = hop(value, "tensor", 1)
     cross = hop(far, "tensor", 1)
     return [value, near, far, cross]
 
 
 def exchange_tensor(pieces):
-    return [pieces[0]] + [hop(pieces[k], "tensor", k) for k in (1, 2, 3)]
+    out = [pieces[0], hop(pieces[1], "tensor", 1)]
+    return out + [hop(pieces[k], "tensor", k) for k in (2, 3)]
 
 
 def scatter_tensor(pieces):
     over = hop(pieces[3].astype(bf16), "tensor", 1)
-    beside = hop(pieces[1].astype(bf16), "tensor", 1)
     outward = (pieces[2].astype(f32) + over.astype(f32)).astype(bf16)
     back = hop(outward, "tensor", 2)
+    beside = hop(pieces[1].astype(bf16), "tensor", 1)
     return pieces[0].astype(f32) + beside.astype(f32) + back.astype(f32)
 
 
@@ -308,11 +407,84 @@
     return lax.psum_scatter(value.astype(bf16), "dp", scatter_dimension=0, tiled=True).astype(f32)
 
 
-def gelu_tanh(pre_value):
-    return jax.nn.gelu(pre_value, approximate=True)
-
-
-def local(
+def gather_dp_steps(value):
+    count = lax.axis_size("dp")
+    if count > 8:
+        return gather_dp(value)
+    place = lax.axis_index("dp")
+    share = value.shape
+    bit = count // 2
+    axis = 0
+    while bit:
+        other = hop(value, "dp", bit)
+        upper = (place & bit) > 0
+        low = jnp.where(upper, other, value)
+        high = jnp.where(upper, value, other)
+        value = jnp.stack([low, high], axis=axis)
+        axis += 1
+        bit //= 2
+    return value.reshape((count * share[0],) + share[1:])
+
+
+def scatter_dp_parts(parts):
+    count = lax.axis_size("dp")
+    parts = parts[:1] + [hop(parts[k], "dp", k) for k in range(1, count)]
+    total = parts[0].astype(f32)
+    for part in parts[1:]:
+        total = total + part.astype(f32)
+    return total
+
+
+def qkv_weights_kernel(place_ref, normed_ref, dqkv_ref, w_ref, other_ref, *refs):
+    parts, gain_ref, acc = refs[:-2], refs[-2], refs[-1]
+    step = pl.program_id(0)
+    cols = acc.shape[1]
+    part = dot(normed_ref[...], dqkv_ref[...], ((0,), (0,)))
+
+    @pl.when(step == 0)
+    def _():
+        acc[...] = part
+
+    @pl.when(step > 0)
+    def _():
+        acc[...] += part
+
+    @pl.when(step == pl.num_programs(0) - 1)
+    def _():
+        gain_ref[...] = jnp.sum(acc[...] * w_ref[...].astype(f32), axis=1, keepdims=True)
+        share = acc.shape[0] // len(parts)
+        for k, ref in enumerate(parts):
+            at = pl.multiple_of((place_ref[0] ^ k) * share, 8)
+            ref[:, :cols] = acc[pl.ds(at, share), :].astype(bf16)
+            ref[:, cols:] = other_ref[pl.ds(at, share), :].astype(bf16)
+
+
+def qkv_weights(normed, dqkv, w, other, place, count):
+    rows, width = normed.shape
+    cols = dqkv.shape[1]
+    extra = other.shape[1]
+    step = 2 * ROW_STEP
+    share = width // count
+    return pl.pallas_call(
+        qkv_weights_kernel,
+        grid=(rows // step,),
+        in_specs=[
+            pl.BlockSpec(memory_space=pltpu.SMEM),
+            pl.BlockSpec((step, width), lambda i: (i, 0)),
+            pl.BlockSpec((step, cols), lambda i: (i, 0)),
+            pl.BlockSpec(w.shape, lambda i: (0, 0)),
+            pl.BlockSpec(other.shape, lambda i: (0, 0)),
+        ],
+        out_specs=[pl.BlockSpec((share, cols + extra), lambda i: (0, 0))] * count
+        + [pl.BlockSpec((width, 1), lambda i: (0, 0))],
+        out_shape=[jax.ShapeDtypeStruct((share, cols + extra), bf16)] * count
+        + [jax.ShapeDtypeStruct((width, 1), f32)],
+        scratch_shapes=[pltpu.VMEM((width, cols), f32)],
+        name="qkv_weights",
+    )(place, normed, dqkv, w, other)
+
+
+def layer(
     hidden_in,
     earlier,
     gain_attn,
@@ -337,11 +509,10 @@
     hidden = hidden_in.astype(f32)
     normed_attn = layer_norm(hidden, gain_attn).astype(bf16)
     attn_pieces = gather_tensor(normed_attn)
-    full_qkv = gather_dp(w_qkv.reshape(shard_d, 3 * head_cols))
+    full_qkv = gather_dp_steps(w_qkv.reshape(shard_d, 3 * head_cols))
     out_pieces = gather_tensor(w_out.T)
     full_out = gather_dp(jnp.concatenate(out_pieces, axis=1))
-    full_up = gather_dp(w_up)
-    full_down_t = gather_dp(w_down.T)
+    updown = gather_dp(jnp.concatenate([w_up, w_down.T], axis=1))
 
     first, position = slot_layout(lengths, slot_len)
     first = first.reshape(slot_count, 1, slot_len)
@@ -350,34 +521,29 @@
     perm_col = perm[:, None]
     perm_row = perm[None, :]
 
-    normed_slot, qkv = project(attn_pieces, perm_col, full_qkv, cosine, sine)
+    cotangent = grad_out.astype(f32)
+    own_grad = mix_weights[4] * cotangent
+    grad_pieces = gather_tensor(own_grad.astype(bf16))
+
+    normed_slot = to_slots(attn_pieces, perm_col)
+    qkv = project(normed_slot, full_qkv, cosine, sine)
     *attended, stat = attend(qkv, first, perm_row, own_rows)
     heads_here = jnp.concatenate(exchange_tensor(attended), axis=1)
     after_attn = hidden + dot(heads_here, full_out, ((1,), (1,)))
     normed_mlp = layer_norm(after_attn, gain_mlp).astype(bf16)
-    mlp_rows = jnp.concatenate(gather_tensor(normed_mlp), axis=0)
-
-    cotangent = grad_out.astype(f32)
-    own_grad = mix_weights[4] * cotangent
-    grad_rows = jnp.concatenate(gather_tensor(own_grad.astype(bf16)), axis=0)
-
-    pre_act = dot(mlp_rows, full_up)
-    activated = gelu_tanh(pre_act).astype(bf16)
-    grad_act = dot(grad_rows, full_down_t)
-    unused_value, gelu_back = jax.vjp(gelu_tanh, pre_act)
-    grad_pre = gelu_back(grad_act)[0].astype(bf16)
-    partial = dot(grad_pre, full_up, ((1,), (1,)))
-    grad_normed_mlp = scatter_tensor(
-        [partial[k * own_rows : (k + 1) * own_rows] for k in range(4)]
-    )
-    partial_out = dot(activated, full_down_t, ((1,), (1,)))
-    block_out = after_attn + scatter_tensor(
-        [partial_out[k * own_rows : (k + 1) * own_rows] for k in range(4)]
-    )
-    grad_down_t = scatter_dp(dot(grad_rows, activated, ((0,), (0,))))
-    grad_up = scatter_dp(dot(mlp_rows, grad_pre, ((0,), (0,))))
-
-    unused_norm, second_back = jax.vjp(layer_norm, after_attn, gain_mlp)
+    mlp_rows = gather_tensor(normed_mlp)
+
+    dn0, hid0, du0, dn1, hid1, du1 = mlp(mlp_rows[:2], grad_pieces[:2], updown)
+    dn2, hid2, du2, dn3, hid3, du3 = mlp(mlp_rows[2:], grad_pieces[2:], updown)
+    grad_normed_mlp = scatter_tensor([dn0, dn1, dn2, dn3])
+    hids = [hid0, hid1, hid2, hid3]
+    mlp_total = scatter_tensor(mlp_out(hids, updown))
+    grad_updown = scatter_dp(mlp_weights(mlp_rows, grad_pieces, hids, [du0, du1, du2, du3]))
+    units = w_up.shape[1]
+    grad_up = grad_updown[:, :units]
+    grad_down_t = grad_updown[:, units:]
+
+    _, second_back = jax.vjp(layer_norm, after_attn, gain_mlp)
     grad_resid_mlp, grad_gain_mlp = second_back(grad_normed_mlp)
     grad_after = own_grad + grad_resid_mlp
     grad_low = grad_after.astype(bf16)
@@ -389,21 +555,37 @@
     out_scattered = scatter_tensor(
         [out_partial[:, k * head_cols : (k + 1) * head_cols] for k in range(4)]
     )
-    grad_out_t = scatter_dp(out_scattered)
-
     dqkv = attend_back(qkv, first, perm_col, grad_attended, stat, cosine, sine)
-    attn_partial = unproject(dqkv, perm_row, full_qkv, own_rows)
-    grad_normed_attn = scatter_tensor(
-        [attn_partial[k * own_rows : (k + 1) * own_rows] for k in range(4)]
-    )
-    qkv_partial = dot(normed_slot, dqkv, ((0,), (0,)))
-    grad_qkv = scatter_dp(qkv_partial)
-    grad_gain_attn = jnp.sum(qkv_partial * full_qkv.astype(f32), axis=1) / gain_attn
-
-    unused_first, first_back = jax.vjp(lambda value: layer_norm(value, gain_attn), hidden)
+    late_attn, late_grad, late_earlier, dqkv = lax.optimization_barrier(
+        (after_attn, grad_out, earlier, dqkv)
+    )
+    part2, part3 = unproject(dqkv, perm_row, full_qkv, own_rows, 2)
+    dp_count = lax.axis_size("dp")
+    small = dp_count <= 8
+    *parts, gain_partial = qkv_weights(
+        normed_slot,
+        dqkv,
+        full_qkv,
+        out_scattered,
+        jnp.full((1,), lax.axis_index("dp") if small else 0, jnp.int32),
+        dp_count if small else 1,
+    )
+    part0, part1 = unproject(dqkv, perm_row, full_qkv, own_rows, 0)
+    grad_normed_attn = scatter_tensor([part0, part1, part2, part3])
+    if small:
+        grad_both = scatter_dp_parts(parts)
+    else:
+        grad_both = scatter_dp(parts[0])
+    grad_qkv = grad_both[:, : 3 * head_cols]
+    grad_out_t = grad_both[:, 3 * head_cols :]
+    grad_gain_attn = gain_partial[:, 0] / gain_attn
+
+    _, first_back = jax.vjp(lambda value: layer_norm(value, gain_attn), hidden)
     grad_hidden = (grad_after + first_back(grad_normed_attn)[0]).astype(bf16)
 
-    prior = [earlier[index].astype(f32) for index in range(4)]
+    cotangent = late_grad.astype(f32)
+    block_out = late_attn + mlp_total
+    prior = [late_earlier[index].astype(f32) for index in range(4)]
     mixed_total = mix_weights[4] * block_out
     for index in range(4):
         mixed_total = mixed_total + mix_weights[index] * prior[index]
@@ -432,7 +614,7 @@
     rows = P(("dp", "tensor"), None)
     layers = P(None, ("dp", "tensor"), None)
     return jax.shard_map(
-        local,
+        layer,
         mesh=mesh,
         in_specs=(
             rows,

time: 516 us -> 370 us (0.72)
  waiting for transfers between devices: 243 us -> 106 us
  matrix products: 47.9 us -> 5.54 us
  Pallas kernels: 71.7 us -> 114 us
  blocking collectives: 37.3 us -> 0 us
  starting transfers between devices: 24.3 us -> 38.9 us
  other arithmetic: 45.1 us -> 57.5 us
    unnamed x9 -> x3, waiting for transfers between devices: 106 us -> 0.05 us
    dot_general x10 -> x3, matrix products: 47.9 us -> 5.54 us  [dot(): return lax.dot_general(a, b, (dims, ((), ())), preferred_element_type=f32)]
    pallas_call x2 -> x9, Pallas kernels: 31.6 us -> 73.3 us  [the longest x2 15.9 us: unproject(): pl.pallas_call(kernel, grid=(each // ROW_STEP,), in_specs=[pl.BlockSpec((...]
    all_gather x1 -> x0, blocking collectives: 37.3 us -> none  [gather_dp(): return lax.all_gather(value, 'dp', axis=0, tiled=True)]
    ppermute x35 -> x45, waiting for transfers between devices: 125 us -> 106 us  [hop(): return lax.ppermute(value, axis, [(i, i ^ bit) for i in range(count)])]
    ppermute x35 -> x45, starting transfers between devices: 23.5 us -> 38.7 us  [hop(): return lax.ppermute(value, axis, [(i, i ^ bit) for i in range(count)])]
    all_gather x3 -> x2, waiting for transfers between devices: 11.4 us -> 0.02 us  [gather_dp(): return lax.all_gather(value, 'dp', axis=0, tiled=True)]
    unnamed x86 -> x95, local copies, waits for them, and re-layouts: 10.9 us -> 8.23 us
  transfers between devices with their start and end apart: 42 -> 48, of which waited for: 21 -> 22; matrix products, arithmetic and copies ran while one was open for 19% -> 22% of each run, Pallas kernels for 14% -> 31%
where the time goes in v2:
time: 370 us; the launch traced here: 363 us
  Pallas kernels  114 us (31%)
  waiting for transfers between devices  106 us (29%)
  other arithmetic  57.5 us (16%)
  starting transfers between devices  38.9 us (11%)
  local copies, waits for them, and re-layouts  26.2 us (7%)
  between operations  14.6 us (4%)
  matrix products  5.54 us (1%)
    ppermute x45, waiting for transfers between devices, hop(): return lax.ppermute(value, axis, [(i, i ^ bit) for i in range(count)])  106 us
    ppermute x45, starting transfers between devices, hop(): return lax.ppermute(value, axis, [(i, i ^ bit) for i in range(count)])  38.7 us
    pallas_call x1, Pallas kernels, attend_back(): pl.pallas_call(attend_back_kernel, grid=(slots,), in_specs=[pl.BlockSpec(...  22.6 us
    pallas_call x1, Pallas kernels, attend(): pl.pallas_call(attend_kernel, grid=(slots,), in_specs=[pl.BlockSpec((leng...  17.9 us
    pallas_call x2, Pallas kernels, unproject(): pl.pallas_call(kernel, grid=(each // ROW_STEP,), in_specs=[pl.BlockSpec((...  15.9 us
    pallas_call x2, Pallas kernels, mlp(): pl.pallas_call(mlp_kernel, grid=(each // ROW_STEP,), in_specs=[block] * 4...  15.9 us
    pallas_call x1, Pallas kernels, to_slots(): pl.pallas_call(order_kernel, grid=(rows // ROW_STEP,), in_specs=[whole] *...  11.1 us
    pallas_call x1, Pallas kernels, mlp_weights(): pl.pallas_call(mlp_weights_kernel, grid=(each // ROW_STEP,), in_specs=[bl...  10.1 us
  transfers between devices with their start and end apart: 48, of which 22 were waited for; matrix products, arithmetic and copies ran while one was open for 22% of the time, Pallas kernels for 31%

profile of v2, /device:TPU:0, one launch (start us, length us, event | category | flops | bytes accessed | tf_op | source)
XLA Modules:
  0.0 362.8 jit_solution(11010704711580209479)
XLA Ops:
  8.2 3.0 collective-permute-start.10
  20.8 2.7 collective-permute-start.3
  24.6 8.0 %collective-permute-done.3 = bf16[96,576]{0,1:T(8,128)(2,1)S(1)} collective-permute-done((bf16[96,576]{0,1:T(8,128)(2,1)S(1)}, bf16[96,576]{0,1:T(8,128)(2,1)S(1)}, u32[]{:S(2)}, u32[]{:S(2)}) %collective-permute-start.3) | collective-permute-done | bytes 110624 | tf_op jit(solution)/shard_map/ppermute | solution.py:370
  35.0 5.3 %fusion.22 = (f32[2048,32]{1,0:T(8,128)S(1)}, f32[2048,32]{1,0:T(8,128)S(1)}, f32[2048,32]{1,0:T(8,128)}) fusion(f32[32]{0:T(128)S(1)} %negate_power_fusion, f32[2048]{0:T(1024)S(1)} %bitcast.86), kind=kLoop, calls=%fused_computation.62 | loop fusion | flops 131072 | bytes 794752 | tf_op jit(solution)/shard_map/neg | solution.py:43
  40.3 3.0 collective-permute-done.4
  51.7 5.7 %pad_maximum_fusion.1 = (f32[2048,128]{1,0:T(8,128)}, f32[2048,128]{1,0:T(8,128)}) fusion(f32[2048,32]{1,0:T(8,128)} %get-tuple-element.162, f32[2048,32]{1,0:T(8,128)S(1)} %get-tuple-element.161, f32[2048,32]{1,0:T(8,128)S(1)} %get-tuple-element.160), kind=kLoop, calls=%fused_computation.51 | loop fusion | flops 1572864 | bytes 2883584 | tf_op jit(solution)/shard_map/concatenate | solution.py:42
  57.4 7.1 %collective-permute-done.5 = bf16[2,2,96,576]{3,2,1,0:T(8,128)(2,1)} collective-permute-done((bf16[2,2,96,576]{3,2,1,0:T(8,128)(2,1)}, bf16[2,2,96,576]{3,2,1,0:T(8,128)(2,1)}, u32[]{:S(2)}, u32[]{:S(2)}) %collective-permute-start.5) | collective-permute-done | bytes 442400 | tf_op jit(solution)/shard_map/ppermute | solution.py:370
  67.7 11.1 %to_slots.1.normed_ref = bf16[2048,768]{1,0:T(8,128)(2,1)} custom-call(bf16[512,768]{1,0:T(8,128)(2,1)} %fusion.16.n0, bf16[512,768]{1,0:T(8,128)(2,1)} %collective-permute-done.n1, bf16[512,768]{1,0:T(8,128)(2,1)} %collective-permute-done.1.n2, bf16[512,768]{1,0:T(8,128)(2,1)} %collective-permute-done.2.n3, s32[2048,1]{1,0:T(8,128)} %copy.67.perm_ref), custom_call_target="tpu_custom_call" | custom-call | tf_op jit(solution)/shard_map/to_slots/pallas_call | solution.py:80
  78.9 6.8 %project.1.qkv_ref = bf16[2048,576]{1,0:T(8,128)(2,1)} custom-call(bf16[2048,768]{1,0:T(8,128)(2,1)} %to_slots.1.normed_ref, bf16[768,576]{1,0:T(8,128)(2,1)} %bitcast.71, f32[2048,128]{1,0:T(8,128)} %get-tuple-element.174.cos_ref, f32[2048,128]{1,0:T(8,128)} %get-tuple-element.175.sin_ref), custom_call_target="tpu_custom_call" | custom-call | tf_op jit(solution)/shard_map/project/pallas_call | solution.py:106
  85.6 17.9 %attend.1 = (bf16[512,192]{1,0:T(8,128)(2,1)}, bf16[512,192]{1,0:T(8,128)(2,1)}, bf16[512,192]{1,0:T(8,128)(2,1)}, bf16[512,192]{1,0:T(8,128)(2,1)}, f32[2,8,1024]{2,1,0:T(8,128)}) custom-call(bf16[2048,576]{1,0:T(8,128)(2,1)} %project.1.qkv_ref, s32[2,1,1024]{2,1,0:T(1,128)} %reshape.129.first_ref, s32[1,2048]{1,0:T(1,128)} %bitcast.78), custom_call_target="tpu_custom_call" | custom-call | tf_op jit(solution)/shard_map/attend/pallas_call | solution.py:263
  108.5 3.8 %collective-permute-done.8 = bf16[512,192]{1,0:T(8,128)(2,1)S(1)} collective-permute-done((bf16[512,192]{1,0:T(8,128)(2,1)}, bf16[512,192]{1,0:T(8,128)(2,1)S(1)}, u32[]{:S(2)}, u32[]{:S(2)}) %collective-permute-start.8) | collective-permute-done | bytes 196640 | tf_op jit(solution)/shard_map/ppermute | solution.py:370
  112.4 5.7 %collective-permute-done.7 = bf16[512,192]{1,0:T(8,128)(2,1)S(1)} collective-permute-done((bf16[512,192]{1,0:T(8,128)(2,1)}, bf16[512,192]{1,0:T(8,128)(2,1)S(1)}, u32[]{:S(2)}, u32[]{:S(2)}) %collective-permute-start.7) | collective-permute-done | bytes 196640 | tf_op jit(solution)/shard_map/ppermute | solution.py:370
  123.7 11.2 %collective-permute-done.17.ga_ref.refs_6_ = bf16[512,768]{1,0:T(8,128)(2,1)} collective-permute-done((bf16[512,768]{1,0:T(8,128)(2,1)}, bf16[512,768]{1,0:T(8,128)(2,1)}, u32[]{:S(2)}, u32[]{:S(2)}) %collective-permute-start.17) | collective-permute-done | bytes 786464 | tf_op jit(solution)/shard_map/ppermute | solution.py:370
  135.0 16.7 %collective-permute-done.15.a_ref.refs_2_ = bf16[512,768]{1,0:T(8,128)(2,1)S(1)} collective-permute-done((bf16[512,768]{1,0:T(8,128)(2,1)}, bf16[512,768]{1,0:T(8,128)(2,1)S(1)}, u32[]{:S(2)}, u32[]{:S(2)}) %collective-permute-start.15) | collective-permute-done | bytes 786464 | tf_op jit(solution)/shard_map/ppermute | solution.py:370
  155.0 7.8 %shard_map.196 = (bf16[512,768]{1,0:T(8,128)(2,1)}, bf16[512,768]{1,0:T(8,128)(2,1)}, bf16[512,768]{1,0:T(8,128)(2,1)}, bf16[512,768]{1,0:T(8,128)(2,1)}, bf16[5...) custom-call(bf16[512,768]{1,0:T(8,128)(2,1)} %copy-done.4, bf16[512,768]{1,0:T(8,128)(2,1)} %collective-permute-done.16.b_ref.refs_3_, ...), custom_call_target="tpu_custom_call" | custom-call | tf_op jit(solution)/shard_map/pallas_call | solution.py:143
  163.1 8.1 %shard_map.195 = (bf16[512,768]{1,0:T(8,128)(2,1)}, bf16[512,768]{1,0:T(8,128)(2,1)}, bf16[512,768]{1,0:T(8,128)(2,1)}, bf16[512,768]{1,0:T(8,128)(2,1)}, bf16[5...) custom-call(bf16[512,768]{1,0:T(8,128)(2,1)} %multiply_convert_fusion.1.a_ref.refs_0_, ...), custom_call_target="tpu_custom_call" | custom-call | tf_op jit(solution)/shard_map/pallas_call | solution.py:143
  171.2 5.6 %mlp_out.1 = (bf16[512,768]{1,0:T(8,128)(2,1)}, bf16[512,768]{1,0:T(8,128)(2,1)}, bf16[512,768]{1,0:T(8,128)(2,1)}, bf16[512,768]{1,0:T(8,128)(2,1)}) custom-call(bf16[512,768]{1,0:T(8,128)(2,1)} %get-tuple-element.58.h0.refs_8_, bf16[512,768]{1,0:T(8,128)(2,1)} %get-tuple-element.59.h1.refs_9_, bf16[512,768]{1,0:T(8,128)(2,1)} %get-tuple-element.60.h2.refs_10_, ...), custom_call_target="tpu_custom_call" | custom-call | tf_op jit(solution)/shard_map/mlp_out/pallas_call | solution.py:164
  180.5 10.1 %mlp_weights.1 = bf16[768,1536]{1,0:T(8,128)(2,1)} custom-call(bf16[512,768]{1,0:T(8,128)(2,1)} %multiply_convert_fusion.1.a_ref.refs_0_, bf16[512,768]{1,0:T(8,128)(2,1)} %collective-permute-done.12.b_ref.refs_1_, bf16[512,768]{1,0:T(8,128)(2,1)} %copy-done.4, bf16[512,768]{1,0:T(8,128)(2,1)} %collective-permute-done.16.b_ref.refs_3_, ...), custom_call_target="tpu_custom_call" | custom-call | tf_op jit(solution)/shard_map/mlp_weights/pallas_call | solution.py:204
  194.6 5.9 %collective-permute-done.20 = bf16[512,768]{1,0:T(8,128)(2,1)} collective-permute-done((bf16[512,768]{1,0:T(8,128)(2,1)}, bf16[512,768]{1,0:T(8,128)(2,1)}, u32[]{:S(2)}, u32[]{:S(2)}) %collective-permute-start.20) | collective-permute-done | bytes 786464 | tf_op jit(solution)/shard_map/ppermute | solution.py:370
  200.5 2.8 multiply_reduce_fusion
  214.6 8.2 %collective-permute-done.22.d2 = bf16[512,192]{1,0:T(8,128)(2,1)S(1)} collective-permute-done((bf16[512,192]{1,0:T(8,128)(2,1)S(1)}, bf16[512,192]{1,0:T(8,128)(2,1)S(1)}, u32[]{:S(2)}, u32[]{:S(2)}) %collective-permute-start.22) | collective-permute-done | bytes 196640 | tf_op jit(solution)/shard_map/ppermute | solution.py:370
  223.6 3.8 %collective-permute-done.23.d3 = bf16[512,192]{1,0:T(8,128)(2,1)} collective-permute-done((bf16[512,192]{1,0:T(8,128)(2,1)S(1)}, bf16[512,192]{1,0:T(8,128)(2,1)}, u32[]{:S(2)}, u32[]{:S(2)}) %collective-permute-start.23) | collective-permute-done | bytes 196640 | tf_op jit(solution)/shard_map/ppermute | solution.py:370
  227.4 22.6 %attend_back.1.dqkv_ref = bf16[2048,576]{1,0:T(8,128)(2,1)} custom-call(bf16[2048,576]{1,0:T(8,128)(2,1)} %project.1.qkv_ref, s32[2,1,1024]{2,1,0:T(1,128)} %reshape.129.first_ref, s32[2048,1]{1,0:T(8,128)} %copy.67.perm_ref, bf16[512,192]{1,0:T(8,128)(2,1)} %get-tuple-element.155.d0, bf16[512,192]{1,0:T(8,128)(2,1)} %copy-done.12, ...), custom_call_target="tpu_custom_call" | custom-call | tf_op jit(solution)/shard_map/attend_back/pallas_call | solution.py:324
  250.0 8.1 %shard_map.198 = (bf16[512,768]{1,0:T(8,128)(2,1)}, bf16[512,768]{1,0:T(8,128)(2,1)}) custom-call(bf16[2048,576]{1,0:T(8,128)(2,1)} %attend_back.1.dqkv_ref, s32[1,2048]{1,0:T(1,128)} %bitcast.79, bf16[768,576]{1,0:T(8,128)(2,1)} %bitcast.72), custom_call_target="tpu_custom_call" | custom-call | tf_op jit(solution)/shard_map/pallas_call | solution.py:355
  261.0 8.5 %fusion.13 = (f32[]{:T(128)}, f32[]{:T(128)}, f32[]{:T(128)}, f32[]{:T(128)}, f32[]{:T(128)}, /*index=5*/bf16[512,768]{1,0:T(8,128)(2,1)}) fusion(bf16[512,768]{1,0:T(8,128)(2,1)S(1)} %copy-done.1, bf16[4,512,768]{2,1,0:T(8,128)(2,1)} %param.13, f32[512,768]{1,0:T(8,128)S(1)} %get-tuple-element.57, bf16[512,768]{1,0:T(8,128)(2,1)} %collective-permute-done.26, ...), kind=kLoop, calls=%fused_computation.28 | loop fusion | flops 12189691 | bytes 8650792 | tf_op jit(solution)/shard_map/reduce_sum | solution.py:593
  273.5 7.9 %qkv_weights.1 = (bf16[96,768]{1,0:T(8,128)(2,1)}, bf16[96,768]{1,0:T(8,128)(2,1)}, bf16[96,768]{1,0:T(8,128)(2,1)}, bf16[96,768]{1,0:T(8,128)(2,1)}, bf16[96,76...) custom-call(s32[1]{0:T(128)} %bitcast.21.place_ref, ...), custom_call_target="tpu_custom_call" | custom-call | tf_op jit(solution)/shard_map/qkv_weights/pallas_call | solution.py:468
  282.6 3.3 concatenate.23
  287.7 3.0 collective-permute-done.34
  291.1 3.3 collective-permute-done.35
  295.6 7.9 %shard_map.197 = (bf16[512,768]{1,0:T(8,128)(2,1)}, bf16[512,768]{1,0:T(8,128)(2,1)}) custom-call(bf16[2048,576]{1,0:T(8,128)(2,1)} %attend_back.1.dqkv_ref, s32[1,2048]{1,0:T(1,128)} %bitcast.80, bf16[768,576]{1,0:T(8,128)(2,1)} %bitcast.74), custom_call_target="tpu_custom_call" | custom-call | tf_op jit(solution)/shard_map/pallas_call | solution.py:355
  314.3 12.5 %collective-permute-done.37 = f32[16,128]{1,0:T(8,128)S(1)} collective-permute-done((f32[16,128]{1,0:T(8,128)S(1)}, f32[16,128]{1,0:T(8,128)S(1)}, u32[]{:S(2)}, u32[]{:S(2)}) %collective-permute-start.37) | collective-permute-done | bytes 8224 | tf_op jit(solution)/shard_map/ppermute | solution.py:370
  331.0 4.0 %collective-permute-start.40 = (bf16[96,768]{1,0:T(8,128)(2,1)S(1)}, bf16[96,768]{1,0:T(8,128)(2,1)S(1)}, u32[]{:S(2)}, u32[]{:S(2)}) collective-permute-start(bf16[96,768]{1,0:T(8,128)(2,1)S(1)} %copy-done.40), channel_id=1, source_target_pairs={{0,12},{4,8},{8,4},{12,0},{16,28},{20,24},{24,20},{28,16},{1,13},{... | collective-permute-start | bytes 442376 | tf_op jit(solution)/shard_map/ppermute | solution.py:370
  (245 shorter events, 106.9 us)
Async XLA Ops:
  7.2 110.8 %all-gather.3.cloned.1.call-start = ((), (), s32[]{:S(2)}) async-start(), calls=%async_computation.1 | async-start | bytes 1327104 | tf_op jit(solution)/shard_map/all_gather | solution.py:403
  15.3 139.7 %all-gather.5.cloned.1.call-start = ((), (), s32[]{:S(2)}) async-start(), calls=%async_computation.2 | async-start | bytes 2654208 | tf_op jit(solution)/shard_map/all_gather | solution.py:403
  18.4 49.3 %collective-permute-start = (bf16[512,768]{1,0:T(8,128)(2,1)}, bf16[512,768]{1,0:T(8,128)(2,1)}, u32[]{:S(2)}, u32[]{:S(2)}) collective-permute-start(bf16[512,768]{1,0:T(8,128)(2,1)} %fusion.16.n0), channel_id=1, source_target_pairs={{0,1},{1,0},{2,3},{3,2},{4,5},{5,4},{6,7},{7,6},{8,9},{9,8},{10,11... | collective-permute-start | bytes 2359304 | tf_op jit(solution)/shard_map/ppermute | solution.py:370
  18.6 32.4 %collective-permute-start.1 = (bf16[512,768]{1,0:T(8,128)(2,1)}, bf16[512,768]{1,0:T(8,128)(2,1)}, u32[]{:S(2)}, u32[]{:S(2)}) collective-permute-start(bf16[512,768]{1,0:T(8,128)(2,1)} %fusion.16.n0), channel_id=1, source_target_pairs={{0,2},{1,3},{2,0},{3,1},{4,6},{5,7},{6,4},{7,5},{8,10},{9,11},{10,... | collective-permute-start | bytes 2359304 | tf_op jit(solution)/shard_map/ppermute | solution.py:370
  20.8 11.8 %collective-permute-start.3 = (bf16[96,576]{0,1:T(8,128)(2,1)S(1)}, bf16[96,576]{0,1:T(8,128)(2,1)S(1)}, u32[]{:S(2)}, u32[]{:S(2)}) collective-permute-start(bf16[96,576]{0,1:T(8,128)(2,1)S(1)} %bitcast.76), channel_id=1, source_target_pairs={{0,16},{4,20},{8,24},{12,28},{16,0},{20,4},{24,8},{28,12},{1,17},{... | collective-permute-start | bytes 331784 | tf_op jit(solution)/shard_map/ppermute | solution.py:370
  24.2 329.4 %reduce-scatter.2.cloned.1.call-start = ((), (), s32[]{:S(2)}) async-start(), calls=%async_computation.3 | async-start | bytes 2654208 | tf_op jit(solution)/shard_map/reduce_scatter | solution.py:407
  32.7 10.6 %collective-permute-start.4 = (bf16[2,96,576]{1,2,0:T(8,128)(2,1)S(1)}, bf16[2,96,576]{1,2,0:T(8,128)(2,1)}, u32[]{:S(2)}, u32[]{:S(2)}) collective-permute-start(bf16[2,96,576]{1,2,0:T(8,128)(2,1)S(1)} %pad_maximum_fusion.5), channel_id=1, source_target_pairs={{0,8},{4,12},{8,0},{12,4},{16,24},{20,28},{24,16},{28,20},{1,9},{5... | collective-permute-start | bytes 663560 | tf_op jit(solution)/shard_map/ppermute | solution.py:370
  47.5 17.1 %collective-permute-start.5 = (bf16[2,2,96,576]{3,2,1,0:T(8,128)(2,1)}, bf16[2,2,96,576]{3,2,1,0:T(8,128)(2,1)}, u32[]{:S(2)}, u32[]{:S(2)}) collective-permute-start(bf16[2,2,96,576]{3,2,1,0:T(8,128)(2,1)} %copy.69), channel_id=1, source_target_pairs={{0,4},{4,0},{8,12},{12,8},{16,20},{20,16},{24,28},{28,24},{1,5},{5... | collective-permute-start | bytes 1327112 | tf_op jit(solution)/shard_map/ppermute | solution.py:370
  51.0 16.7 %collective-permute-start.2 = (bf16[512,768]{1,0:T(8,128)(2,1)}, bf16[512,768]{1,0:T(8,128)(2,1)}, u32[]{:S(2)}, u32[]{:S(2)}) collective-permute-start(bf16[512,768]{1,0:T(8,128)(2,1)} %collective-permute-done.1.n2), channel_id=1, source_target_pairs={{0,1},{1,0},{2,3},{3,2},{4,5},{5,4},{6,7},{7,6},{8,9},{9,8},{10,11... | collective-permute-start | bytes 2359304 | tf_op jit(solution)/shard_map/ppermute | solution.py:370
  104.1 14.0 %collective-permute-start.7 = (bf16[512,192]{1,0:T(8,128)(2,1)}, bf16[512,192]{1,0:T(8,128)(2,1)S(1)}, u32[]{:S(2)}, u32[]{:S(2)}) collective-permute-start(bf16[512,192]{1,0:T(8,128)(2,1)} %get-tuple-element.50), channel_id=1, source_target_pairs={{0,2},{1,3},{2,0},{3,1},{4,6},{5,7},{6,4},{7,5},{8,10},{9,11},{10,... | collective-permute-start | bytes 589832 | tf_op jit(solution)/shard_map/ppermute | solution.py:370
  105.1 12.9 %collective-permute-start.6 = (bf16[512,192]{1,0:T(8,128)(2,1)}, bf16[512,192]{1,0:T(8,128)(2,1)S(1)}, u32[]{:S(2)}, u32[]{:S(2)}) collective-permute-start(bf16[512,192]{1,0:T(8,128)(2,1)} %get-tuple-element.49), channel_id=1, source_target_pairs={{0,1},{1,0},{2,3},{3,2},{4,5},{5,4},{6,7},{7,6},{8,9},{9,8},{10,11... | collective-permute-start | bytes 589832 | tf_op jit(solution)/shard_map/ppermute | solution.py:370
  107.1 27.9 %collective-permute-start.17 = (bf16[512,768]{1,0:T(8,128)(2,1)}, bf16[512,768]{1,0:T(8,128)(2,1)}, u32[]{:S(2)}, u32[]{:S(2)}) collective-permute-start(bf16[512,768]{1,0:T(8,128)(2,1)} %fusion.18.ga_ref.refs_4_), channel_id=1, source_target_pairs={{0,2},{1,3},{2,0},{3,1},{4,6},{5,7},{6,4},{7,5},{8,10},{9,11},{10,... | collective-permute-start | bytes 2359304 | tf_op jit(solution)/shard_map/ppermute | solution.py:370
  123.1 28.6 %collective-permute-start.15 = (bf16[512,768]{1,0:T(8,128)(2,1)}, bf16[512,768]{1,0:T(8,128)(2,1)S(1)}, u32[]{:S(2)}, u32[]{:S(2)}) collective-permute-start(bf16[512,768]{1,0:T(8,128)(2,1)} %multiply_convert_fusion.1.a_ref.refs_0_), channel_id=1, source_target_pairs={{0,2},{1,3},{2,0},{3,1},{4,6},{5,7},{6,4},{7,5},{8,10},{9,11},{10,... | collective-permute-start | bytes 2359304 | tf_op jit(solution)/shard_map/ppermute | solution.py:370
  135.0 18.2 %collective-permute-start.18 = (bf16[512,768]{1,0:T(8,128)(2,1)}, bf16[512,768]{1,0:T(8,128)(2,1)}, u32[]{:S(2)}, u32[]{:S(2)}) collective-permute-start(bf16[512,768]{1,0:T(8,128)(2,1)} %collective-permute-done.17.ga_ref.refs_6_), channel_id=1, source_target_pairs={{0,1},{1,0},{2,3},{3,2},{4,5},{5,4},{6,7},{7,6},{8,9},{9,8},{10,11... | collective-permute-start | bytes 2359304 | tf_op jit(solution)/shard_map/ppermute | solution.py:370
  162.9 14.5 %collective-permute-start.19 = (bf16[512,768]{1,0:T(8,128)(2,1)}, bf16[512,768]{1,0:T(8,128)(2,1)}, u32[]{:S(2)}, u32[]{:S(2)}) collective-permute-start(bf16[512,768]{1,0:T(8,128)(2,1)} %get-tuple-element.55), channel_id=1, source_target_pairs={{0,1},{1,0},{2,3},{3,2},{4,5},{5,4},{6,7},{7,6},{8,9},{9,8},{10,11... | collective-permute-start | bytes 2359304 | tf_op jit(solution)/shard_map/ppermute | solution.py:370
  176.8 13.9 %collective-permute-start.25 = (bf16[512,768]{1,0:T(8,128)(2,1)}, bf16[512,768]{1,0:T(8,128)(2,1)}, u32[]{:S(2)}, u32[]{:S(2)}) collective-permute-start(bf16[512,768]{1,0:T(8,128)(2,1)} %get-tuple-element.65), channel_id=1, source_target_pairs={{0,1},{1,0},{2,3},{3,2},{4,5},{5,4},{6,7},{7,6},{8,9},{9,8},{10,11... | collective-permute-start | bytes 2359304 | tf_op jit(solution)/shard_map/ppermute | solution.py:370
  177.2 17.4 %collective-permute-start.14 = (bf16[512,768]{1,0:T(8,128)(2,1)}, bf16[512,768]{1,0:T(8,128)(2,1)}, u32[]{:S(2)}, u32[]{:S(2)}) collective-permute-start(bf16[512,768]{1,0:T(8,128)(2,1)} %get-tuple-element.53), channel_id=1, source_target_pairs={{0,1},{1,0},{2,3},{3,2},{4,5},{5,4},{6,7},{7,6},{8,9},{9,8},{10,11... | collective-permute-start | bytes 2359304 | tf_op jit(solution)/shard_map/ppermute | solution.py:370
  179.8 20.7 %collective-permute-start.20 = (bf16[512,768]{1,0:T(8,128)(2,1)}, bf16[512,768]{1,0:T(8,128)(2,1)}, u32[]{:S(2)}, u32[]{:S(2)}) collective-permute-start(bf16[512,768]{1,0:T(8,128)(2,1)} %add_convert_fusion.3), channel_id=1, source_target_pairs={{0,2},{1,3},{2,0},{3,1},{4,6},{5,7},{6,4},{7,5},{8,10},{9,11},{10,... | collective-permute-start | bytes 2359304 | tf_op jit(solution)/shard_map/ppermute | solution.py:370
  180.5 80.5 %collective-permute-start.24 = (bf16[512,768]{1,0:T(8,128)(2,1)}, bf16[512,768]{1,0:T(8,128)(2,1)}, u32[]{:S(2)}, u32[]{:S(2)}) collective-permute-start(bf16[512,768]{1,0:T(8,128)(2,1)} %get-tuple-element.63), channel_id=1, source_target_pairs={{0,1},{1,0},{2,3},{3,2},{4,5},{5,4},{6,7},{7,6},{8,9},{9,8},{10,11... | collective-permute-start | bytes 2359304 | tf_op jit(solution)/shard_map/ppermute | solution.py:370
  193.2 67.8 %collective-permute-start.26 = (bf16[512,768]{1,0:T(8,128)(2,1)}, bf16[512,768]{1,0:T(8,128)(2,1)}, u32[]{:S(2)}, u32[]{:S(2)}) collective-permute-start(bf16[512,768]{1,0:T(8,128)(2,1)} %add_convert_fusion.2), channel_id=1, source_target_pairs={{0,2},{1,3},{2,0},{3,1},{4,6},{5,7},{6,4},{7,5},{8,10},{9,11},{10,... | collective-permute-start | bytes 2359304 | tf_op jit(solution)/shard_map/ppermute | solution.py:370
  212.8 46.1 %collective-permute-start.31 = (bf16[768,192]{1,0:T(8,128)(2,1)}, bf16[768,192]{1,0:T(8,128)(2,1)}, u32[]{:S(2)}, u32[]{:S(2)}) collective-permute-start(bf16[768,192]{1,0:T(8,128)(2,1)} %get-tuple-element.149), channel_id=1, source_target_pairs={{0,1},{1,0},{2,3},{3,2},{4,5},{5,4},{6,7},{7,6},{8,9},{9,8},{10,11... | collective-permute-start | bytes 884744 | tf_op jit(solution)/shard_map/ppermute | solution.py:370
  213.8 13.6 %collective-permute-start.23 = (bf16[512,192]{1,0:T(8,128)(2,1)S(1)}, bf16[512,192]{1,0:T(8,128)(2,1)}, u32[]{:S(2)}, u32[]{:S(2)}) collective-permute-start(bf16[512,192]{1,0:T(8,128)(2,1)S(1)} %get-tuple-element.152), channel_id=1, source_target_pairs={{0,3},{1,2},{2,1},{3,0},{4,7},{5,6},{6,5},{7,4},{8,11},{9,10},{10,... | collective-permute-start | bytes 589832 | tf_op jit(solution)/shard_map/ppermute | solution.py:370
  223.6 45.9 %collective-permute-start.30 = (bf16[768,192]{1,0:T(8,128)(2,1)}, bf16[768,192]{1,0:T(8,128)(2,1)S(1)}, u32[]{:S(2)}, u32[]{:S(2)}) collective-permute-start(bf16[768,192]{1,0:T(8,128)(2,1)} %get-tuple-element.148), channel_id=1, source_target_pairs={{0,1},{1,0},{2,3},{3,2},{4,5},{5,4},{6,7},{7,6},{8,9},{9,8},{10,11... | collective-permute-start | bytes 884744 | tf_op jit(solution)/shard_map/ppermute | solution.py:370
  258.1 51.7 %collective-permute-start.28 = (bf16[512,768]{1,0:T(8,128)(2,1)}, bf16[512,768]{1,0:T(8,128)(2,1)}, u32[]{:S(2)}, u32[]{:S(2)}) collective-permute-start(bf16[512,768]{1,0:T(8,128)(2,1)} %get-tuple-element.71), channel_id=1, source_target_pairs={{0,1},{1,0},{2,3},{3,2},{4,5},{5,4},{6,7},{7,6},{8,9},{9,8},{10,11... | collective-permute-start | bytes 2359304 | tf_op jit(solution)/shard_map/ppermute | solution.py:370
  260.2 11.2 %collective-permute-start.32 = (bf16[768,192]{1,0:T(8,128)(2,1)S(1)}, bf16[768,192]{1,0:T(8,128)(2,1)S(1)}, u32[]{:S(2)}, u32[]{:S(2)}) collective-permute-start(bf16[768,192]{1,0:T(8,128)(2,1)S(1)} %fusion.20), channel_id=1, source_target_pairs={{0,2},{1,3},{2,0},{3,1},{4,6},{5,7},{6,4},{7,5},{8,10},{9,11},{10,... | collective-permute-start | bytes 884744 | tf_op jit(solution)/shard_map/ppermute | solution.py:370
  294.3 13.9 %collective-permute-start.36 = (f32[16,128]{1,0:T(8,128)S(1)}, f32[16,128]{1,0:T(8,128)S(1)}, u32[]{:S(2)}, u32[]{:S(2)}) collective-permute-start(f32[16,128]{1,0:T(8,128)S(1)} %add.156), channel_id=1, source_target_pairs={{0,8},{4,12},{8,0},{12,4},{16,24},{20,28},{24,16},{28,20},{1,9},{5... | collective-permute-start | bytes 24584 | tf_op jit(solution)/shard_map/ppermute | solution.py:370
  303.7 44.0 %collective-permute-start.27 = (bf16[512,768]{1,0:T(8,128)(2,1)}, bf16[512,768]{1,0:T(8,128)(2,1)S(1)}, u32[]{:S(2)}, u32[]{:S(2)}) collective-permute-start(bf16[512,768]{1,0:T(8,128)(2,1)} %get-tuple-element.69), channel_id=1, source_target_pairs={{0,1},{1,0},{2,3},{3,2},{4,5},{5,4},{6,7},{7,6},{8,9},{9,8},{10,11... | collective-permute-start | bytes 2359304 | tf_op jit(solution)/shard_map/ppermute | solution.py:370
  304.4 22.4 %collective-permute-start.44 = (bf16[96,768]{1,0:T(8,128)(2,1)S(1)}, bf16[96,768]{1,0:T(8,128)(2,1)S(1)}, u32[]{:S(2)}, u32[]{:S(2)}) collective-permute-start(bf16[96,768]{1,0:T(8,128)(2,1)S(1)} %copy-done.44), channel_id=1, source_target_pairs={{0,28},{4,24},{8,20},{12,16},{16,12},{20,8},{24,4},{28,0},{1,29},{... | collective-permute-start | bytes 442376 | tf_op jit(solution)/shard_map/ppermute | solution.py:370
  306.8 24.2 %collective-permute-start.43 = (bf16[96,768]{1,0:T(8,128)(2,1)S(1)}, bf16[96,768]{1,0:T(8,128)(2,1)S(1)}, u32[]{:S(2)}, u32[]{:S(2)}) collective-permute-start(bf16[96,768]{1,0:T(8,128)(2,1)S(1)} %copy-done.43), channel_id=1, source_target_pairs={{0,24},{4,28},{8,16},{12,20},{16,8},{20,12},{24,0},{28,4},{1,25},{... | collective-permute-start | bytes 442376 | tf_op jit(solution)/shard_map/ppermute | solution.py:370
  308.2 26.8 %collective-permute-start.42 = (bf16[96,768]{1,0:T(8,128)(2,1)S(1)}, bf16[96,768]{1,0:T(8,128)(2,1)S(1)}, u32[]{:S(2)}, u32[]{:S(2)}) collective-permute-start(bf16[96,768]{1,0:T(8,128)(2,1)S(1)} %copy-done.42), channel_id=1, source_target_pairs={{0,20},{4,16},{8,28},{12,24},{16,4},{20,0},{24,12},{28,8},{1,21},{... | collective-permute-start | bytes 442376 | tf_op jit(solution)/shard_map/ppermute | solution.py:370
  309.8 17.0 %collective-permute-start.37 = (f32[16,128]{1,0:T(8,128)S(1)}, f32[16,128]{1,0:T(8,128)S(1)}, u32[]{:S(2)}, u32[]{:S(2)}) collective-permute-start(f32[16,128]{1,0:T(8,128)S(1)} %add.157), channel_id=1, source_target_pairs={{0,16},{4,20},{8,24},{12,28},{16,0},{20,4},{24,8},{28,12},{1,17},{... | collective-permute-start | bytes 24584 | tf_op jit(solution)/shard_map/ppermute | solution.py:370
  326.8 20.9 %collective-permute-start.29 = (bf16[512,768]{1,0:T(8,128)(2,1)}, bf16[512,768]{1,0:T(8,128)(2,1)}, u32[]{:S(2)}, u32[]{:S(2)}) collective-permute-start(bf16[512,768]{1,0:T(8,128)(2,1)} %add_convert_fusion.1), channel_id=1, source_target_pairs={{0,2},{1,3},{2,0},{3,1},{4,6},{5,7},{6,4},{7,5},{8,10},{9,11},{10,... | collective-permute-start | bytes 2359304 | tf_op jit(solution)/shard_map/ppermute | solution.py:370
  (61 other events, 393.7 us)
Sparse Core Ops, SparseCore 0:
  15.4 48.4 all-gather.2
  66.6 51.9 all-gather.4
  190.8 69.5 reduce-scatter.1
